TPU v7x, 1024 devices: a whole 4x8x16 slice. The times are simulated.
1024 devices in a mesh: seq: 4 (over x), exp: 32 (over z, core), head: 8 (over y).
Axes of the slice: x: 4, y: 8, z: 16, core: 2. Of those that a mesh axis runs over, the one named last changes fastest.
Arguments:
- out_grad: bfloat16 [12288, 2048], P(('exp', 'head')), may hold values from -6 to 6
- layer_input: bfloat16 [12288, 2048], P(('exp', 'head')), may hold values from -6 to 6
- norm_gain: float32 [2048], replicated, may hold values from 0.5 to 1.5
- routes: int32 [12288, 8], P(('exp', 'head')), may hold values from 0 to 63, all different within a row; in each aligned block of 48 rows (0 to 47, 48 to 95, ...) at most 8 rows name the same one
- gates: float32 [12288, 8], P(('exp', 'head')), may hold values from 0.02 to 0.3
- gate_pre: bfloat16 [8, 64, 32, 8, 768], P('head', 'exp', None, None, 'seq'), may hold values from -6 to 6
- up_pre: bfloat16 [8, 64, 32, 8, 768], P('head', 'exp', None, None, 'seq'), may hold values from -6 to 6
- w_gate: bfloat16 [64, 2048, 768], P('exp', None, 'seq'), may hold values from -0.125 to 0.125
- w_up: bfloat16 [64, 2048, 768], P('exp', None, 'seq'), may hold values from -0.125 to 0.125
- w_down: bfloat16 [64, 768, 2048], P('exp', 'seq'), may hold values from -0.21875 to 0.21875
- w_out: bfloat16 [4096, 2048], P('head'), may hold values from -0.09375 to 0.09375
Outputs:
- resid_grad: float32 [4, 3072, 2048], P('seq', ('exp', 'head'))
- head_grad: bfloat16 [4, 3072, 4096], P('seq', 'exp', 'head')
Inputs may be any that keep to these rules, and one draw needn't show every extreme that they name: `routes`: each row names 8 different experts. In each aligned block of 48 rows (the tokens of one device) no expert is named by more than 8 rows, a bound that some block reaches.
All inputs are finite; a program needn't handle non-finite values.
Results may differ from a plain program's by a relative error of at most 0.0095.
Values may be sent and summed in bfloat16 or wider, within the bound.
No kernel may reach another device: no remote copies, remote signals or barrier semaphores. Data moves between devices by JAX's collectives and lax.ppermute only.
A program may use at most 32 MiB of HBM per device.

v0:
```python
import jax
import jax.numpy as jnp
from jax import lax
from jax.sharding import PartitionSpec as P


def expert_rows(slot_piece, gate_piece, up_piece, w_gate, w_up, w_down):
    gate_act = gate_piece.astype(jnp.float32)
    up_act = up_piece.astype(jnp.float32)
    d_hidden = jnp.einsum("jgcd,jfd->jgcf", slot_piece, w_down, preferred_element_type=jnp.float32)
    sigmoid_gate = jax.nn.sigmoid(gate_act)
    silu_gate = gate_act * sigmoid_gate
    silu_slope = sigmoid_gate * (1.0 + gate_act * (1.0 - sigmoid_gate))
    d_gate = (d_hidden * up_act * silu_slope).astype(jnp.bfloat16)
    d_up = (d_hidden * silu_gate).astype(jnp.bfloat16)
    partial_value = jnp.einsum("jgcf,jdf->jgcd", d_gate, w_gate, preferred_element_type=jnp.float32)
    partial_value = partial_value + jnp.einsum(
        "jgcf,jdf->jgcd", d_up, w_up, preferred_element_type=jnp.float32
    )
    return partial_value.astype(jnp.bfloat16)


def shards(
    out_grad, layer_input, norm_gain, routes, gates, gate_pre, up_pre, w_gate, w_up, w_down, w_out
):
    experts_here = w_gate.shape[0]
    exp_groups = lax.axis_size("exp")
    capacity = gate_pre.shape[3]
    tok_count = routes.shape[0]
    top_count = routes.shape[1]
    model_width = out_grad.shape[1]
    total_experts = experts_here * exp_groups
    flat_routes = routes.reshape(-1)
    onehot = (flat_routes[:, None] == jnp.arange(total_experts, dtype=jnp.int32)[None, :]).astype(
        jnp.int32
    )
    position = jnp.sum((jnp.cumsum(onehot, axis=0) - 1) * onehot, axis=1)
    target = flat_routes // experts_here
    local_expert = flat_routes % experts_here
    slot_index = (local_expert * exp_groups + target) * capacity + position
    scaled = (
        (gates[:, :, None] * out_grad[:, None, :].astype(jnp.float32))
        .astype(jnp.bfloat16)
        .reshape(-1, model_width)
    )
    outgoing = (
        jnp.zeros((total_experts * capacity, model_width), jnp.bfloat16).at[slot_index].set(scaled)
    )
    outgoing = outgoing.reshape(experts_here, exp_groups, capacity, model_width)
    gate_local = gate_pre[0]
    up_local = up_pre[0]
    received = lax.all_to_all(outgoing, "exp", split_axis=1, concat_axis=1, tiled=True)
    partial_value = expert_rows(received, gate_local, up_local, w_gate, w_up, w_down)
    returned = lax.all_to_all(
        partial_value, "exp", split_axis=1, concat_axis=1, tiled=True
    ).reshape(-1, model_width)
    picked = returned[slot_index].astype(jnp.float32)
    combined = jnp.sum(picked.reshape(tok_count, top_count, model_width), axis=1)
    moe_rows = lax.psum_scatter(
        combined.astype(jnp.bfloat16), "seq", scatter_dimension=0, tiled=True
    ).astype(jnp.float32)
    rows_here = moe_rows.shape[0]
    row_start = lax.axis_index("seq") * rows_here
    inputs = lax.dynamic_slice_in_dim(layer_input, row_start, rows_here, 0).astype(jnp.float32)
    out_rows = lax.dynamic_slice_in_dim(out_grad, row_start, rows_here, 0).astype(jnp.float32)
    inv_rms = lax.rsqrt(jnp.mean(inputs * inputs, axis=1, keepdims=True) + 1e-06)
    normed = inputs * inv_rms
    scaled_grad = moe_rows * norm_gain[None, :]
    resid_grad = out_rows + inv_rms * (
        scaled_grad - normed * jnp.mean(scaled_grad * normed, axis=1, keepdims=True)
    )
    rounded_grad = resid_grad.astype(jnp.bfloat16)
    head_grad = lax.dot_general(
        lax.all_gather(rounded_grad, "head", axis=0, tiled=True),
        w_out,
        (((1,), (1,)), ((), ())),
        preferred_element_type=jnp.float32,
    )
    return (resid_grad[None], head_grad.astype(jnp.bfloat16)[None])


def solution(mesh):
    placed = (
        P(("exp", "head"), None),
        P(("exp", "head"), None),
        P(),
        P(("exp", "head"), None),
        P(("exp", "head"), None),
        P("head", "exp", None, None, "seq"),
        P("head", "exp", None, None, "seq"),
        P("exp", None, "seq"),
        P("exp", None, "seq"),
        P("exp", "seq", None),
        P("head", None),
    )
    return jax.shard_map(
        shards,
        mesh=mesh,
        in_specs=placed,
        out_specs=(P("seq", ("exp", "head"), None), P("seq", "exp", "head")),
        check_vma=False,
    )
```

profile of v0, /device:TPU:2, one launch (start us, length us, event | category | flops | bytes accessed | tf_op | source)
XLA Modules:
  0.0 304.8 jit_solution(9052687949796206958)
XLA Ops:
  0.6 0.9 copy.27
  1.9 0.9 reduce-window.6
  3.0 1.0 convert_element_type.55
  4.0 0.8 copy.31
  5.0 4.5 %scatter_custom_fusion = bf16[512,2048]{1,0:T(8,128)(2,1)} fusion(s32[384]{0:T(512)S(1)} %fusion.40, f32[48,2048]{1,0:T(8,128)S(1)} %convert_element_type.55, f32[384]{0:T(512)S(1)} %mul.112, bf16[]{:T(256)} %constant.55.clone.1), kind=kCustom, calls=%fused_computation.7 | custom fusion | flops 1572864 | bytes 2492418 | tf_op jit(solution)/shard_map/scatter | solution.py:47
  9.5 1.7 copy.32
  11.2 120.0 %all_to_all.10 = bf16[2,32,8,2048]{3,2,0,1:T(8,128)(2,1)S(1)} all-to-all(bf16[2,32,8,2048]{3,2,0,1:T(8,128)(2,1)S(1)} %copy.32), channel_id=1, replica_groups=mesh['seq'=4,'exp'=32,'head'=8] {'exp'}, dimensions={1} | all-to-all | bytes 4194304 | tf_op jit(solution)/shard_map/all_to_all | solution.py:52
  131.3 0.8 fusion.2
  132.8 0.8 fusion.7
  134.2 0.8 add_convert_fusion
  134.9 1.5 copy.34
  136.5 4.9 %all-to-all-start.1 = ((bf16[2,32,8,2048]{3,2,0,1:T(8,128)(2,1)}), bf16[2,32,8,2048]{3,2,0,1:T(8,128)(2,1)}, u32[]{:S(2)}, u32[]{:S(2)}) async-start(bf16[2,32,8,2048]{3,2,0,1:T(8,128)(2,1)} %copy.34), calls=%async_computation.1 | async-start | bytes 4194304 | tf_op jit(solution)/shard_map/all_to_all | solution.py:54
  141.6 101.2 %all-to-all-done.1 = bf16[2,32,8,2048]{3,2,0,1:T(8,128)(2,1)} async-done(((bf16[2,32,8,2048]{3,2,0,1:T(8,128)(2,1)}), bf16[2,32,8,2048]{3,2,0,1:T(8,128)(2,1)}, u32[]{:S(2)}, u32[]{:S(2)}) %all-to-all-start.1) | async-done | bytes 2097184 | tf_op jit(solution)/shard_map/all_to_all | solution.py:54
  242.8 3.1 %copy.35 = bf16[2,32,8,2048]{3,2,1,0:T(8,128)(2,1)} copy(bf16[2,32,8,2048]{3,2,0,1:T(8,128)(2,1)} %all-to-all-done.1) | data formatting | bytes 4194304 | tf_op jit(solution)/shard_map/all_to_all | solution.py:54
  245.9 6.9 %gather_fusion = bf16[384,2048]{1,0:T(8,128)(2,1)} fusion(bf16[512,2048]{1,0:T(8,128)(2,1)} %bitcast.67, s32[1024]{0:T(1024)S(1)} %pad_clamp_fusion), kind=kCustom, calls=%fused_computation | custom fusion | bytes 3147264 | tf_op jit(solution)/shard_map/gather | solution.py:57
  252.9 2.5 bitcast_reduce_fusion
  255.3 12.7 %fusion = bf16[16,2048]{1,0:T(8,128)(2,1)S(1)} fusion(bf16[48,2048]{1,0:T(8,128)(2,1)S(1)} %bitcast_reduce_fusion), kind=kCustom, calls=%all-reduce-scatter | all-reduce-scatter fusion | flops 131073 | bytes 266240
  268.1 2.1 collective-permute-start
  270.2 1.3 dynamic-slice.4
  272.1 2.1 collective-permute-done
  274.7 1.0 convert_bitcast_fusion
  275.7 26.9 %all-gather = bf16[8,12,2048]{2,1,0:T(8,128)(2,1)S(1)} all-gather(bf16[1,12,2048]{2,1,0:T(8,128)(2,1)S(1)} %get-tuple-element.6), channel_id=1, replica_groups=mesh['seq'=4,'exp'=32,'head'=8] {'head'}, dimensions={0}, use_global_device_ids=true | all-gather | bytes 442368 | tf_op jit(solution)/shard_map/all_gather | solution.py:74
  302.6 0.7 copy.36
  303.4 1.4 fusion.12
  (33 shorter events, 2.8 us)
Async XLA Ops:
  0.6 302.7 %copy-start = (bf16[512,2048]{1,0:T(8,128)(2,1)S(1)}, bf16[512,2048]{1,0:T(8,128)(2,1)}, u32[]{:S(2)}) copy-start(bf16[512,2048]{1,0:T(8,128)(2,1)} %param.21) | copy-start | bytes 6291460
  11.2 120.0 %copy-start.7 = (bf16[2,192,2048]{2,1,0:T(8,128)(2,1)S(1)}, bf16[2,192,2048]{2,1,0:T(8,128)(2,1)}, u32[]{:S(2)}) copy-start(bf16[2,192,2048]{2,1,0:T(8,128)(2,1)} %param.20) | copy-start | bytes 4718596
  131.3 1.4 copy-start.1
  131.3 1.4 copy-start.3
  131.3 1.5 copy-start.4
  132.8 1.4 copy-start.2
  136.5 4.9 %copy-start.5 = (bf16[48,2048]{1,0:T(8,128)(2,1)S(1)}, bf16[48,2048]{1,0:T(8,128)(2,1)}, u32[]{:S(2)}) copy-start(bf16[48,2048]{1,0:T(8,128)(2,1)} %param.12) | copy-start | bytes 589828
  136.5 106.3 %all-to-all-start.1 = ((bf16[2,32,8,2048]{3,2,0,1:T(8,128)(2,1)}), bf16[2,32,8,2048]{3,2,0,1:T(8,128)(2,1)}, u32[]{:S(2)}, u32[]{:S(2)}) async-start(bf16[2,32,8,2048]{3,2,0,1:T(8,128)(2,1)} %copy.34), calls=%async_computation.1 | async-start | bytes 4194304 | tf_op jit(solution)/shard_map/all_to_all | solution.py:54
  252.9 21.6 %copy-start.6 = (f32[2048]{0:T(1024)S(1)}, f32[2048]{0:T(1024)}, u32[]{:S(2)}) copy-start(f32[2048]{0:T(1024)} %param.13) | copy-start | bytes 24580
  268.1 6.2 %collective-permute-start = (bf16[12,2048]{1,0:T(8,128)(2,1)S(1)}, bf16[12,2048]{1,0:T(8,128)(2,1)S(1)}, u32[]{:S(2)}, u32[]{:S(2)}) collective-permute-start(bf16[12,2048]{1,0:T(8,128)(2,1)S(1)} %slice.11), channel_id=1, source_target_pairs={{0,256},{256,512},{512,768},{1,257},{257,513},{513,769},{2,258},{2... | collective-permute-start | bytes 147464
where the time goes:
time: 305 us
  blocking collectives  160 us (52%)
  waiting for transfers between devices  103 us (34%)
  local copies, waits for them, and re-layouts  19.2 us (6%)
  other arithmetic  10.4 us (3%)
  starting transfers between devices  6.98 us (2%)
  matrix products  3.79 us (1%)
    all_to_all x1, blocking collectives, shards(): lax.all_to_all(outgoing, 'exp', split_axis=1, concat_axis=1, tiled=True)  120 us
    all_to_all x1, waiting for transfers between devices, shards(): lax.all_to_all(partial_value, 'exp', split_axis=1, concat_axis=1, tiled=T...  101 us
    all_gather x1, blocking collectives, shards(): lax.all_gather(rounded_grad, 'head', axis=0, tiled=True)  26.9 us
    unnamed x1, blocking collectives  12.7 us
    gather x1, local copies, waits for them, and re-layouts, shards(): picked = returned[slot_index].astype(jnp.float32)  6.93 us
  transfers between devices with their start and end apart: 2, of which 2 were waited for; matrix products, arithmetic and copies ran while one was open for 0% of the time, Pallas kernels for 0%

commit v1 on v0

v1 whole, which is shorter than its diff:
```python
import functools

import jax
import jax.numpy as jnp
from jax import lax
from jax.experimental import pallas as pl
from jax.experimental.pallas import tpu as pltpu
from jax.sharding import PartitionSpec as P

BF = jnp.bfloat16
F32 = jnp.float32
I32 = jnp.int32
VM = pl.BlockSpec(memory_space=pltpu.VMEM)
SM = pl.BlockSpec(memory_space=pltpu.SMEM)
PAD = 16
LANES = 128
GRANT = 24 << 20


def iota(shape, dim):
    return lax.broadcasted_iota(I32, shape, dim)


def one_hot(where):
    return jnp.where(where, 1.0, 0.0).astype(BF)


def dot(a, b):
    return jnp.dot(a, b, preferred_element_type=F32)


def dot_t(a, b):
    return lax.dot_general(a, b, (((1,), (1,)), ((), ())), preferred_element_type=F32)


def dispatch_kernel(capacity, quarter_ref, routes_ref, gates_ref, grad_ref, slots_ref, pick_ref):
    top, tok_count = routes_ref.shape
    rows, piece = slots_ref.shape
    start = pl.multiple_of(quarter_ref[0] * piece, piece)
    cols = grad_ref[:, pl.ds(start, piece)]
    square = (tok_count, tok_count)
    earlier = one_hot(iota(square, 0) < iota(square, 1))
    row = iota((rows, tok_count), 0)
    expert = row // capacity
    named = jnp.zeros((rows, tok_count), F32)
    gate = jnp.zeros((rows, tok_count), F32)
    for k in range(top):
        hit = routes_ref[k : k + 1, :] == expert
        named = jnp.where(hit, 1.0, named)
        gate = jnp.where(hit, gates_ref[k : k + 1, :], gate)
    count = dot(named.astype(BF), earlier)
    here = (named > 0.0) & (count == (row % capacity).astype(F32))
    weight = jnp.sum(jnp.where(here, gate, 0.0), axis=1, keepdims=True)
    pick = one_hot(here)
    pick_ref[...] = pick
    slots_ref[...] = (dot(pick, cols) * weight).astype(BF)


def hidden_kernel(quarter_ref, rows_ref, *refs):
    downs, out_ref = refs[:-1], refs[-1]
    groups, block, piece = rows_ref.shape
    experts_here, hidden, _ = downs[0].shape
    capacity = block // experts_here
    quarters = len(downs)
    wide = rows_ref[...].astype(F32)
    for j in range(experts_here):
        mine = wide[:, j * capacity : (j + 1) * capacity, :]
        mine = mine.reshape(groups * capacity, piece).astype(BF)
        for d in range(quarters):
            target = lax.rem(quarter_ref[0] + quarters - d, quarters)
            value = dot_t(downs[d][j], mine)
            out_ref[target, j * hidden : (j + 1) * hidden, :] = value.astype(BF)


def expert_kernel(parts_ref, gate_ref, up_ref, wg_ref, wu_ref, out_ref):
    quarters, groups, block, piece = out_ref.shape
    experts_here, hidden, _ = wg_ref.shape
    capacity = block // experts_here
    rows = groups * capacity
    grads = []
    for j in range(experts_here):
        band = slice(j * hidden, (j + 1) * hidden)
        total = parts_ref[0, band, :].astype(F32)
        for c in range(1, quarters):
            total = total + parts_ref[c, band, :].astype(F32)
        d_hidden = total.T
        act = gate_ref[j].astype(F32)
        up = up_ref[j].astype(F32)
        sig = jax.nn.sigmoid(act)
        d_gate = (d_hidden * up * (sig * (1.0 + act * (1.0 - sig)))).astype(BF)
        d_up = (d_hidden * (act * sig)).astype(BF)
        grads.append((d_gate, d_up))
    for c in range(quarters):
        cols = slice(c * piece, (c + 1) * piece)
        values = []
        for j in range(experts_here):
            value = dot(grads[j][0], wg_ref[j, :, cols]) + dot(grads[j][1], wu_ref[j, :, cols])
            values.append(value.reshape(groups, capacity, piece))
        out_ref[c] = jnp.concatenate(values, axis=1).astype(BF)


def sum_kernel(parts_ref, out_ref):
    total = parts_ref[0].astype(F32)
    for c in range(1, parts_ref.shape[0]):
        total = total + parts_ref[c].astype(F32)
    out_ref[...] = total.astype(BF)


def combine_kernel(pick_ref, back_ref, out_ref):
    quarters, heads, packed, lanes = out_ref.shape
    tok_count = pick_ref.shape[1]
    part = tok_count // quarters
    tiles = packed // part
    total = lax.dot_general(
        pick_ref[...], back_ref[...], (((0,), (0,)), ((), ())), preferred_element_type=F32
    ).astype(BF)
    to = iota((packed, tok_count), 0)
    token = iota((packed, tok_count), 1)
    for c in range(quarters):
        value = jnp.zeros((packed, lanes), F32)
        for n in range(tiles):
            move = one_hot((to // part == n) & (c * part + to % part == token))
            value = value + dot(move, total[:, n * lanes : (n + 1) * lanes])
        value = value.astype(BF)
        for h in range(heads):
            out_ref[c, h] = value


def offset(index, heads):
    turned = jnp.zeros_like(index)
    step = 1
    while step < heads:
        turned = turned * 2 + index // step % 2
        step *= 2
    return turned


def finish_kernel(head_ref, moe_ref, pairs_ref, gain_ref, w_ref, resid_ref, grad_ref, moe):
    quarters, heads, packed, lanes = moe_ref.shape
    part, width = resid_ref.shape
    tiles = packed // part
    piece = tiles * lanes
    rows = heads * PAD
    me = head_ref[0]
    row = iota((rows, heads * packed), 0)
    source = offset(row // PAD, heads) ^ me
    item = iota((rows, heads * packed), 1)
    for n in range(tiles):
        want = source * packed + n * part + row % PAD
        move = one_hot((want == item) & (row % PAD < part))
        for c in range(quarters):
            block = moe_ref[c].reshape(heads * packed, lanes)
            start = c * piece + n * lanes
            moe[:, start : start + lanes] = dot(move, block)
    row = iota((rows, heads * 2 * part), 0)
    item = iota((rows, heads * 2 * part), 1)
    first = (row // PAD) * (2 * part) + row % PAD
    real = row % PAD < part
    pairs = pairs_ref[...]
    x = dot(one_hot((item == first) & real), pairs)
    inv_rms = lax.rsqrt(jnp.sum(x * x, axis=1, keepdims=True) / width + 1e-06)
    normed = x * inv_rms
    scaled = moe[...] * gain_ref[...]
    mean = jnp.sum(scaled * normed, axis=1, keepdims=True) / width
    out_rows = dot(one_hot((item == first + part) & real), pairs)
    full = out_rows + inv_rms * (scaled - normed * mean)
    resid_ref[...] = full[:part]
    product = dot_t(full.astype(BF), w_ref[...]).astype(BF)
    want = iota((heads * part, rows), 0)
    have = iota((heads * part, rows), 1)
    keep = one_hot(offset((want // part) ^ me, heads) * PAD + want % part == have)
    grad_ref[...] = dot(keep, product).astype(BF)


def call(kernel, out_shape, specs, flops, moved, scratch=()):
    return pl.pallas_call(
        kernel,
        out_shape=out_shape,
        in_specs=specs,
        out_specs=jax.tree.map(lambda _: VM, out_shape),
        scratch_shapes=scratch,
        cost_estimate=pl.CostEstimate(flops=flops, bytes_accessed=moved, transcendentals=0),
        compiler_params=pltpu.CompilerParams(vmem_limit_bytes=GRANT),
    )


def exchange(blocks, axis):
    return lax.all_to_all(blocks, axis, split_axis=0, concat_axis=0, tiled=True)


def shards(
    out_grad, layer_input, norm_gain, routes, gates, gate_pre, up_pre, w_gate, w_up, w_down, w_out
):
    experts_here = w_gate.shape[0]
    exp_groups = lax.axis_size("exp")
    quarters = lax.axis_size("seq")
    heads = lax.axis_size("head")
    capacity = gate_pre.shape[3]
    hidden = gate_pre.shape[4]
    tok_count, width = out_grad.shape
    piece = width // quarters
    part = tok_count // quarters
    block = experts_here * capacity
    rows = exp_groups * block
    attn = w_out.shape[0]
    packed = part * piece // LANES
    sds = jax.ShapeDtypeStruct
    quarter = lax.axis_index("seq").astype(I32).reshape(1)
    head = lax.axis_index("head").astype(I32).reshape(1)

    slots, pick = call(
        functools.partial(dispatch_kernel, capacity),
        [sds((rows, piece), BF), sds((rows, tok_count), BF)],
        [SM, VM, VM, VM],
        2 * rows * tok_count * piece,
        1 << 20,
    )(quarter, routes.T, gates.T, out_grad)

    received = exchange(slots.reshape(exp_groups, block, piece), "exp")

    downs = []
    for d in range(quarters):
        start = lax.rem(quarter[0] + d, quarters) * piece
        own = lax.dynamic_slice_in_dim(w_down, start, piece, 2)
        ring = [(i, (i + d) % quarters) for i in range(quarters)]
        downs.append(lax.ppermute(own, "seq", ring) if d else own)

    def own_rows(values):
        return lax.dynamic_slice_in_dim(values, quarter[0] * part, part, 0)

    def doubled(values, step):
        other = lax.ppermute(values, "head", [(i, i ^ step) for i in range(heads)])
        return jnp.concatenate([values, other], axis=0)

    pairs = jnp.concatenate([own_rows(layer_input), own_rows(out_grad)], axis=0)
    pairs = doubled(pairs, heads // 2)
    downs, pairs = lax.optimization_barrier((downs, pairs))

    partial_hidden = call(
        hidden_kernel,
        sds((quarters, experts_here * hidden, exp_groups * capacity), BF),
        [SM] + [VM] * (1 + quarters),
        2 * rows * width * hidden,
        3 << 20,
    )(quarter, received, *downs)
    summands = exchange(partial_hidden, "seq")
    parts = call(
        expert_kernel,
        sds((quarters, exp_groups, block, piece), BF),
        [VM] * 5,
        4 * rows * hidden * width,
        6 << 20,
    )(
        summands,
        gate_pre.reshape(experts_here, exp_groups * capacity, hidden),
        up_pre.reshape(experts_here, exp_groups * capacity, hidden),
        jnp.swapaxes(w_gate, 1, 2),
        jnp.swapaxes(w_up, 1, 2),
    )
    mine = exchange(parts, "seq")
    if heads > 2:
        pairs = doubled(pairs, heads // 4)
    mine, pairs = lax.optimization_barrier((mine, pairs))
    summed = call(
        sum_kernel, sds((exp_groups, block, piece), BF), [VM], 4 * rows * piece, 3 << 20
    )(mine)
    back = exchange(summed, "exp")
    step = heads // 8
    while step > 0:
        pairs = doubled(pairs, step)
        step //= 2
    back, pairs = lax.optimization_barrier((back, pairs))
    combined = call(
        combine_kernel,
        sds((quarters, heads, packed, LANES), BF),
        [VM] * 2,
        2 * rows * tok_count * piece,
        1 << 20,
    )(pick, back.reshape(rows, piece))
    got = exchange(combined.reshape(quarters * heads, packed, LANES), ("seq", "head"))
    resid, head_grad = call(
        finish_kernel,
        [sds((part, width), F32), sds((heads * part, attn), BF)],
        [SM] + [VM] * 4,
        2 * heads * PAD * width * attn,
        4 << 20,
        [pltpu.VMEM((heads * PAD, width), F32)],
    )(head, got.reshape(quarters, heads, packed, LANES), pairs, norm_gain[None, :], w_out)
    return resid[None], head_grad[None]


def solution(mesh):
    placed = (
        P(("exp", "head"), None),
        P(("exp", "head"), None),
        P(),
        P(("exp", "head"), None),
        P(("exp", "head"), None),
        P("head", "exp", None, None, "seq"),
        P("head", "exp", None, None, "seq"),
        P("exp", None, "seq"),
        P("exp", None, "seq"),
        P("exp", "seq", None),
        P("head", None),
    )
    return jax.shard_map(
        shards,
        mesh=mesh,
        in_specs=placed,
        out_specs=(P("seq", ("exp", "head"), None), P("seq", "exp", "head")),
        check_vma=False,
    )
```

time: 305 us -> 179 us (0.59)
  the two profiles are of different devices: /device:TPU:2 before, /device:TPU:8 now
where the time goes in v1:
time: 179 us; the launch traced here: 178 us
  waiting for transfers between devices  77.6 us (43%)
  starting transfers between devices  62.2 us (35%)
  blocking collectives  16.5 us (9%)
  Pallas kernels  11 us (6%)
  local copies, waits for them, and re-layouts  8.02 us (4%)
  other arithmetic  1.82 us (1%)
    all_to_all x4, waiting for transfers between devices, exchange(): return lax.all_to_all(blocks, axis, split_axis=0, concat_axis=0, tiled=True)  54.3 us
    all_to_all x4, starting transfers between devices, exchange(): return lax.all_to_all(blocks, axis, split_axis=0, concat_axis=0, tiled=True)  37 us
    ppermute x3, waiting for transfers between devices, doubled(): other = lax.ppermute(values, 'head', [(i, i ^ step) for i in range(heads)])  23.3 us
    all_to_all x1, blocking collectives, exchange(): return lax.all_to_all(blocks, axis, split_axis=0, concat_axis=0, tiled=True)  16.5 us
    ppermute x3, starting transfers between devices, doubled(): other = lax.ppermute(values, 'head', [(i, i ^ step) for i in range(heads)])  13.8 us
    ppermute x3, starting transfers between devices, shards(): downs.append(lax.ppermute(own, 'seq', ring) if d else own)  11.4 us
    unnamed x33, local copies, waits for them, and re-layouts  5.54 us
  transfers between devices with their start and end apart: 10, of which 7 were waited for; matrix products, arithmetic and copies ran while one was open for 2% of the time, Pallas kernels for 0%

profile of v1, /device:TPU:8, one launch (start us, length us, event | category | flops | bytes accessed | tf_op | source)
XLA Modules:
  0.0 178.1 jit_solution(11738531923156229220)
XLA Ops:
  3.0 1.4 shard_map.122
  5.1 19.2 %all-to-all-start = ((bf16[32,16,512]{2,1,0:T(8,128)(2,1)}), bf16[32,16,512]{2,1,0:T(8,128)(2,1)S(1)}, u32[]{:S(2)}, u32[]{:S(2)}) async-start(bf16[32,16,512]{2,1,0:T(8,128)(2,1)} %bitcast.4), calls=%async_computation | async-start | bytes 1048576 | tf_op jit(solution)/shard_map/all_to_all | solution.py:188
  24.3 1.5 constant_dynamic-slice_fusion.2
  25.8 3.4 %collective-permute-start = (bf16[2,192,512]{2,1,0:T(8,128)(2,1)S(1)}, bf16[2,192,512]{2,1,0:T(8,128)(2,1)S(1)}, u32[]{:S(2)}, u32[]{:S(2)}) collective-permute-start(bf16[2,192,512]{2,1,0:T(8,128)(2,1)S(1)} %get-tuple-element.31), channel_id=1, source_target_pairs={{0,256},{256,512},{512,768},{768,0},{1,257},{257,513},{513,769},{7... | collective-permute-start | bytes 1179656 | tf_op jit(solution)/shard_map/ppermute | solution.py:226
  29.2 4.6 %collective-permute-start.1 = (bf16[2,192,512]{2,1,0:T(8,128)(2,1)S(1)}, bf16[2,192,512]{2,1,0:T(8,128)(2,1)S(1)}, u32[]{:S(2)}, u32[]{:S(2)}) collective-permute-start(bf16[2,192,512]{2,1,0:T(8,128)(2,1)S(1)} %get-tuple-element.33), channel_id=1, source_target_pairs={{0,512},{256,768},{512,0},{768,256},{1,513},{257,769},{513,1},{769... | collective-permute-start | bytes 1179656 | tf_op jit(solution)/shard_map/ppermute | solution.py:226
  33.8 3.3 %collective-permute-start.2 = (bf16[2,192,512]{2,1,0:T(8,128)(2,1)S(1)}, bf16[2,192,512]{2,1,0:T(8,128)(2,1)S(1)}, u32[]{:S(2)}, u32[]{:S(2)}) collective-permute-start(bf16[2,192,512]{2,1,0:T(8,128)(2,1)S(1)} %get-tuple-element.30), channel_id=1, source_target_pairs={{0,768},{256,0},{512,256},{768,512},{1,769},{257,1},{513,257},{769... | collective-permute-start | bytes 1179656 | tf_op jit(solution)/shard_map/ppermute | solution.py:226
  38.2 6.8 %collective-permute-start.3 = (bf16[24,2048]{1,0:T(8,128)(2,1)S(1)}, bf16[24,2048]{1,0:T(8,128)(2,1)S(1)}, u32[]{:S(2)}, u32[]{:S(2)}) collective-permute-start(bf16[24,2048]{1,0:T(8,128)(2,1)S(1)} %pad_maximum_fusion.3), channel_id=1, source_target_pairs={{0,4},{1,5},{2,6},{3,7},{4,0},{5,1},{6,2},{7,3},{8,12},{9,13},{10,... | collective-permute-start | bytes 294920 | tf_op jit(solution)/shard_map/ppermute | solution.py:232
  45.0 5.5 %collective-permute-done.3 = bf16[24,2048]{1,0:T(8,128)(2,1)S(1)} collective-permute-done((bf16[24,2048]{1,0:T(8,128)(2,1)S(1)}, bf16[24,2048]{1,0:T(8,128)(2,1)S(1)}, u32[]{:S(2)}, u32[]{:S(2)}) %collective-permute-start.3) | collective-permute-done | bytes 98336 | tf_op jit(solution)/shard_map/ppermute | solution.py:232
  52.1 6.0 %all-to-all-done.rows_ref = bf16[32,16,512]{2,1,0:T(8,128)(2,1)S(1)} async-done(((bf16[32,16,512]{2,1,0:T(8,128)(2,1)}), bf16[32,16,512]{2,1,0:T(8,128)(2,1)S(1)}, u32[]{:S(2)}, u32[]{:S(2)}) %all-to-all-start) | async-done | bytes 524320 | tf_op jit(solution)/shard_map/all_to_all | solution.py:188
  59.9 16.5 %all_to_all.25.parts_ref = bf16[4,384,256]{2,1,0:T(8,128)(2,1)S(1)} all-to-all(bf16[4,384,256]{2,1,0:T(8,128)(2,1)S(1)} %shard_map.123), channel_id=1, replica_groups=mesh['seq'=4,'exp'=32,'head'=8] {'seq'}, dimensions={0} | all-to-all | bytes 1572864 | tf_op jit(solution)/shard_map/all_to_all | solution.py:188
  76.4 2.8 %shard_map.124 = bf16[4,32,16,512]{3,2,1,0:T(8,128)(2,1)} custom-call(bf16[4,384,256]{2,1,0:T(8,128)(2,1)S(1)} %all_to_all.25.parts_ref, bf16[2,256,192]{2,1,0:T(8,128)(2,1)S(1)} %bitcast.18, bf16[2,256,192]{2,1,0:T(8,128)(2,1)S(1)} %bitcast.19, bf16[2,192,2048]{2,1,0:T(8,128)(2,1)S(1)} %bitcast.15, bf16[2,192,2048]{2,1,0:T(8,128)(2,1)S(1)} %bitcast.16), custom_call_target="tpu_custom_call" | custom-call | flops 805306368 | bytes 6291456 | tf_op jit(solution)/shard_map/pallas_call | solution.py:247
  79.2 3.7 %all-to-all-start.2 = ((bf16[4,32,16,512]{3,2,1,0:T(8,128)(2,1)}), bf16[4,32,16,512]{3,2,1,0:T(8,128)(2,1)S(1)}, u32[]{:S(2)}, u32[]{:S(2)}) async-start(bf16[4,32,16,512]{3,2,1,0:T(8,128)(2,1)} %shard_map.124), calls=%async_computation.2 | async-start | bytes 4194304 | tf_op jit(solution)/shard_map/all_to_all | solution.py:188
  83.0 4.5 %collective-permute-start.4 = (bf16[48,2048]{1,0:T(8,128)(2,1)S(1)}, bf16[48,2048]{1,0:T(8,128)(2,1)S(1)}, u32[]{:S(2)}, u32[]{:S(2)}) collective-permute-start(bf16[48,2048]{1,0:T(8,128)(2,1)S(1)} %copy-done.15), channel_id=1, source_target_pairs={{0,2},{1,3},{2,0},{3,1},{4,6},{5,7},{6,4},{7,5},{8,10},{9,11},{10,... | collective-permute-start | bytes 589832 | tf_op jit(solution)/shard_map/ppermute | solution.py:232
  87.5 7.0 %collective-permute-done.4 = bf16[48,2048]{1,0:T(8,128)(2,1)S(1)} collective-permute-done((bf16[48,2048]{1,0:T(8,128)(2,1)S(1)}, bf16[48,2048]{1,0:T(8,128)(2,1)S(1)}, u32[]{:S(2)}, u32[]{:S(2)}) %collective-permute-start.4) | collective-permute-done | bytes 196640 | tf_op jit(solution)/shard_map/ppermute | solution.py:232
  94.5 13.8 %all-to-all-done.2.parts_ref = bf16[4,32,16,512]{3,2,1,0:T(8,128)(2,1)S(1)} async-done(((bf16[4,32,16,512]{3,2,1,0:T(8,128)(2,1)}), bf16[4,32,16,512]{3,2,1,0:T(8,128)(2,1)S(1)}, u32[]{:S(2)}, u32[]{:S(2)}) %all-to-all-start.2) | async-done | bytes 2097184 | tf_op jit(solution)/shard_map/all_to_all | solution.py:188
  108.3 1.1 shard_map.125
  109.4 5.8 %all-to-all-start.3 = ((bf16[32,16,512]{2,1,0:T(8,128)(2,1)}), bf16[32,16,512]{2,1,0:T(8,128)(2,1)}, u32[]{:S(2)}, u32[]{:S(2)}) async-start(bf16[32,16,512]{2,1,0:T(8,128)(2,1)} %shard_map.125), calls=%async_computation.3 | async-start | bytes 1048576 | tf_op jit(solution)/shard_map/all_to_all | solution.py:188
  115.2 2.5 %collective-permute-start.5 = (bf16[96,2048]{1,0:T(8,128)(2,1)S(1)}, bf16[96,2048]{1,0:T(8,128)(2,1)S(1)}, u32[]{:S(2)}, u32[]{:S(2)}) collective-permute-start(bf16[96,2048]{1,0:T(8,128)(2,1)S(1)} %pad_maximum_fusion.1), channel_id=1, source_target_pairs={{0,1},{1,0},{2,3},{3,2},{4,5},{5,4},{6,7},{7,6},{8,9},{9,8},{10,11... | collective-permute-start | bytes 1179656 | tf_op jit(solution)/shard_map/ppermute | solution.py:232
  117.7 10.8 %collective-permute-done.5 = bf16[96,2048]{1,0:T(8,128)(2,1)S(1)} collective-permute-done((bf16[96,2048]{1,0:T(8,128)(2,1)S(1)}, bf16[96,2048]{1,0:T(8,128)(2,1)S(1)}, u32[]{:S(2)}, u32[]{:S(2)}) %collective-permute-start.5) | collective-permute-done | bytes 393248 | tf_op jit(solution)/shard_map/ppermute | solution.py:232
  129.5 19.4 %all-to-all-done.3 = bf16[32,16,512]{2,1,0:T(8,128)(2,1)} async-done(((bf16[32,16,512]{2,1,0:T(8,128)(2,1)}), bf16[32,16,512]{2,1,0:T(8,128)(2,1)}, u32[]{:S(2)}, u32[]{:S(2)}) %all-to-all-start.3) | async-done | bytes 524320 | tf_op jit(solution)/shard_map/all_to_all | solution.py:188
  149.0 2.3 %shard_map.126 = bf16[4,8,48,128]{3,2,1,0:T(8,128)(2,1)} custom-call(bf16[512,48]{1,0:T(8,128)(2,1)S(1)} %copy-done.10, bf16[512,512]{1,0:T(8,128)(2,1)} %bitcast.9.back_ref), custom_call_target="tpu_custom_call" | custom-call | flops 25165824 | bytes 1048576 | tf_op jit(solution)/shard_map/pallas_call | solution.py:273
  151.2 8.3 %all-to-all-start.4 = ((bf16[32,48,128]{2,1,0:T(8,128)(2,1)}), bf16[32,48,128]{2,1,0:T(8,128)(2,1)S(1)}, u32[]{:S(2)}, u32[]{:S(2)}) async-start(bf16[32,48,128]{2,1,0:T(8,128)(2,1)} %bitcast.10), calls=%async_computation.4 | async-start | bytes 786432 | tf_op jit(solution)/shard_map/all_to_all | solution.py:188
  159.5 15.2 %all-to-all-done.4 = bf16[32,48,128]{2,1,0:T(8,128)(2,1)S(1)} async-done(((bf16[32,48,128]{2,1,0:T(8,128)(2,1)}), bf16[32,48,128]{2,1,0:T(8,128)(2,1)S(1)}, u32[]{:S(2)}, u32[]{:S(2)}) %all-to-all-start.4) | async-done | bytes 393248 | tf_op jit(solution)/shard_map/all_to_all | solution.py:188
  174.7 2.6 %shard_map.127 = (f32[12,2048]{1,0:T(8,128)S(1)}, bf16[96,512]{1,0:T(8,128)(2,1)}) custom-call(s32[1]{0:T(128)} %bitcast.head_ref, bf16[4,8,48,128]{3,2,1,0:T(8,128)(2,1)S(1)} %bitcast.17, bf16[192,2048]{1,0:T(8,128)(2,1)S(1)} %pad_maximum_fusion.pairs_ref, f32[1,2048]{1,0:T(1,128)S(1)} %bitcast.21, bf16[512,2048]{1,0:T(8,128)(2,1)S(1)} %copy-done.1), custom_call_target="tpu_custom_call" | custom-call | flops 268435456 | bytes 4194304 | tf_op jit(solution)/shard_map/pallas_call | solution.py:281
  (43 shorter events, 9.2 us)
Async XLA Ops:
  0.6 37.5 %copy-start = (bf16[48,2048]{1,0:T(8,128)(2,1)S(1)}, bf16[48,2048]{1,0:T(8,128)(2,1)}, u32[]{:S(2)}) copy-start(bf16[48,2048]{1,0:T(8,128)(2,1)} %param.12) | copy-start | bytes 589828
  0.7 1.0 copy-start.6
  1.6 0.7 copy-start.12
  5.1 52.9 %all-to-all-start = ((bf16[32,16,512]{2,1,0:T(8,128)(2,1)}), bf16[32,16,512]{2,1,0:T(8,128)(2,1)S(1)}, u32[]{:S(2)}, u32[]{:S(2)}) async-start(bf16[32,16,512]{2,1,0:T(8,128)(2,1)} %bitcast.4), calls=%async_computation | async-start | bytes 1048576 | tf_op jit(solution)/shard_map/all_to_all | solution.py:188
  25.8 25.5 %collective-permute-start = (bf16[2,192,512]{2,1,0:T(8,128)(2,1)S(1)}, bf16[2,192,512]{2,1,0:T(8,128)(2,1)S(1)}, u32[]{:S(2)}, u32[]{:S(2)}) collective-permute-start(bf16[2,192,512]{2,1,0:T(8,128)(2,1)S(1)} %get-tuple-element.31), channel_id=1, source_target_pairs={{0,256},{256,512},{512,768},{768,0},{1,257},{257,513},{513,769},{7... | collective-permute-start | bytes 1179656 | tf_op jit(solution)/shard_map/ppermute | solution.py:226
  29.2 22.1 %collective-permute-start.1 = (bf16[2,192,512]{2,1,0:T(8,128)(2,1)S(1)}, bf16[2,192,512]{2,1,0:T(8,128)(2,1)S(1)}, u32[]{:S(2)}, u32[]{:S(2)}) collective-permute-start(bf16[2,192,512]{2,1,0:T(8,128)(2,1)S(1)} %get-tuple-element.33), channel_id=1, source_target_pairs={{0,512},{256,768},{512,0},{768,256},{1,513},{257,769},{513,1},{769... | collective-permute-start | bytes 1179656 | tf_op jit(solution)/shard_map/ppermute | solution.py:226
  33.8 17.4 %collective-permute-start.2 = (bf16[2,192,512]{2,1,0:T(8,128)(2,1)S(1)}, bf16[2,192,512]{2,1,0:T(8,128)(2,1)S(1)}, u32[]{:S(2)}, u32[]{:S(2)}) collective-permute-start(bf16[2,192,512]{2,1,0:T(8,128)(2,1)S(1)} %get-tuple-element.30), channel_id=1, source_target_pairs={{0,768},{256,0},{512,256},{768,512},{1,769},{257,1},{513,257},{769... | collective-permute-start | bytes 1179656 | tf_op jit(solution)/shard_map/ppermute | solution.py:226
  38.2 12.4 %collective-permute-start.3 = (bf16[24,2048]{1,0:T(8,128)(2,1)S(1)}, bf16[24,2048]{1,0:T(8,128)(2,1)S(1)}, u32[]{:S(2)}, u32[]{:S(2)}) collective-permute-start(bf16[24,2048]{1,0:T(8,128)(2,1)S(1)} %pad_maximum_fusion.3), channel_id=1, source_target_pairs={{0,4},{1,5},{2,6},{3,7},{4,0},{5,1},{6,2},{7,3},{8,12},{9,13},{10,... | collective-permute-start | bytes 294920 | tf_op jit(solution)/shard_map/ppermute | solution.py:232
  51.3 0.8 copy-start.4
  52.1 24.4 %copy-start.2 = (bf16[2,2048,192]{1,2,0:T(8,128)(2,1)S(1)}, bf16[2,2048,192]{1,2,0:T(8,128)(2,1)}, u32[]{:S(2)}) copy-start(bf16[2,2048,192]{1,2,0:T(8,128)(2,1)} %param.18) | copy-start | bytes 4718596
  58.0 1.0 copy-start.5
  59.0 17.4 %copy-start.3 = (bf16[2,2048,192]{1,2,0:T(8,128)(2,1)S(1)}, bf16[2,2048,192]{1,2,0:T(8,128)(2,1)}, u32[]{:S(2)}) copy-start(bf16[2,2048,192]{1,2,0:T(8,128)(2,1)} %param.19) | copy-start | bytes 4718596
  59.0 17.4 %copy-start.7 = (bf16[1,2,32,8,192]{4,3,2,1,0:T(8,128)(2,1)S(1)}, bf16[1,2,32,8,192]{4,3,2,1,0:T(8,128)(2,1)}, u32[]{:S(2)}) copy-start(bf16[1,2,32,8,192]{4,3,2,1,0:T(8,128)(2,1)} %param.16) | copy-start | bytes 589828
  59.0 17.4 %copy-start.8 = (bf16[1,2,32,8,192]{4,3,2,1,0:T(8,128)(2,1)S(1)}, bf16[1,2,32,8,192]{4,3,2,1,0:T(8,128)(2,1)}, u32[]{:S(2)}) copy-start(bf16[1,2,32,8,192]{4,3,2,1,0:T(8,128)(2,1)} %param.17) | copy-start | bytes 589828
  79.2 3.8 %copy-start.15 = (bf16[48,2048]{1,0:T(8,128)(2,1)S(1)}, bf16[48,2048]{1,0:T(8,128)(2,1)}, u32[]{:S(2)}) copy-start(bf16[48,2048]{1,0:T(8,128)(2,1)} %pad_maximum_fusion.2) | copy-start | bytes 589828
  79.2 29.1 %all-to-all-start.2 = ((bf16[4,32,16,512]{3,2,1,0:T(8,128)(2,1)}), bf16[4,32,16,512]{3,2,1,0:T(8,128)(2,1)S(1)}, u32[]{:S(2)}, u32[]{:S(2)}) async-start(bf16[4,32,16,512]{3,2,1,0:T(8,128)(2,1)} %shard_map.124), calls=%async_computation.2 | async-start | bytes 4194304 | tf_op jit(solution)/shard_map/all_to_all | solution.py:188
  83.0 11.5 %collective-permute-start.4 = (bf16[48,2048]{1,0:T(8,128)(2,1)S(1)}, bf16[48,2048]{1,0:T(8,128)(2,1)S(1)}, u32[]{:S(2)}, u32[]{:S(2)}) collective-permute-start(bf16[48,2048]{1,0:T(8,128)(2,1)S(1)} %copy-done.15), channel_id=1, source_target_pairs={{0,2},{1,3},{2,0},{3,1},{4,6},{5,7},{6,4},{7,5},{8,10},{9,11},{10,... | collective-permute-start | bytes 589832 | tf_op jit(solution)/shard_map/ppermute | solution.py:232
  94.5 20.7 %copy-start.14 = (bf16[96,2048]{1,0:T(8,128)(2,1)}, bf16[96,2048]{1,0:T(8,128)(2,1)S(1)}, u32[]{:S(2)}) copy-start(bf16[96,2048]{1,0:T(8,128)(2,1)S(1)} %pad_maximum_fusion.1) | copy-start | bytes 1179652
  109.4 39.6 %copy-start.10 = (bf16[512,48]{1,0:T(8,128)(2,1)S(1)}, bf16[512,48]{1,0:T(8,128)(2,1)}, u32[]{:S(2)}) copy-start(bf16[512,48]{1,0:T(8,128)(2,1)} %copy-done.9) | copy-start | bytes 147460
  109.4 39.6 %all-to-all-start.3 = ((bf16[32,16,512]{2,1,0:T(8,128)(2,1)}), bf16[32,16,512]{2,1,0:T(8,128)(2,1)}, u32[]{:S(2)}, u32[]{:S(2)}) async-start(bf16[32,16,512]{2,1,0:T(8,128)(2,1)} %shard_map.125), calls=%async_computation.3 | async-start | bytes 1048576 | tf_op jit(solution)/shard_map/all_to_all | solution.py:188
  115.2 59.5 %copy-start.1 = (bf16[512,2048]{1,0:T(8,128)(2,1)S(1)}, bf16[512,2048]{1,0:T(8,128)(2,1)}, u32[]{:S(2)}) copy-start(bf16[512,2048]{1,0:T(8,128)(2,1)} %w_ref.1) | copy-start | bytes 6291460
  115.2 59.5 %copy-start.11 = (f32[2048]{0:T(1024)S(1)}, f32[2048]{0:T(1024)}, u32[]{:S(2)}) copy-start(f32[2048]{0:T(1024)} %param.13) | copy-start | bytes 24580
  115.2 13.2 %collective-permute-start.5 = (bf16[96,2048]{1,0:T(8,128)(2,1)S(1)}, bf16[96,2048]{1,0:T(8,128)(2,1)S(1)}, u32[]{:S(2)}, u32[]{:S(2)}) collective-permute-start(bf16[96,2048]{1,0:T(8,128)(2,1)S(1)} %pad_maximum_fusion.1), channel_id=1, source_target_pairs={{0,1},{1,0},{2,3},{3,2},{4,5},{5,4},{6,7},{7,6},{8,9},{9,8},{10,11... | collective-permute-start | bytes 1179656 | tf_op jit(solution)/shard_map/ppermute | solution.py:232
  151.2 23.5 %all-to-all-start.4 = ((bf16[32,48,128]{2,1,0:T(8,128)(2,1)}), bf16[32,48,128]{2,1,0:T(8,128)(2,1)S(1)}, u32[]{:S(2)}, u32[]{:S(2)}) async-start(bf16[32,48,128]{2,1,0:T(8,128)(2,1)} %bitcast.10), calls=%async_computation.4 | async-start | bytes 786432 | tf_op jit(solution)/shard_map/all_to_all | solution.py:188
  (2 other events, 1.4 us)

commit v2 on v1

--- a/solution.py
+++ b/solution.py
@@ -12,9 +12,11 @@
 I32 = jnp.int32
 VM = pl.BlockSpec(memory_space=pltpu.VMEM)
 SM = pl.BlockSpec(memory_space=pltpu.SMEM)
+HB = pl.BlockSpec(memory_space=pltpu.HBM)
+DMA = pltpu.SemaphoreType.DMA
 PAD = 16
 LANES = 128
-GRANT = 24 << 20
+GRANT = 12 << 20
 
 
 def iota(shape, dim):
@@ -33,27 +35,48 @@
     return lax.dot_general(a, b, (((1,), (1,)), ((), ())), preferred_element_type=F32)
 
 
-def dispatch_kernel(capacity, quarter_ref, routes_ref, gates_ref, grad_ref, slots_ref, pick_ref):
-    top, tok_count = routes_ref.shape
-    rows, piece = slots_ref.shape
-    start = pl.multiple_of(quarter_ref[0] * piece, piece)
-    cols = grad_ref[:, pl.ds(start, piece)]
+def slot_hits(routes, capacity, rows):
+    top, tok_count = routes.shape
     square = (tok_count, tok_count)
     earlier = one_hot(iota(square, 0) < iota(square, 1))
     row = iota((rows, tok_count), 0)
-    expert = row // capacity
+    hits = [routes[k : k + 1, :] == row // capacity for k in range(top)]
     named = jnp.zeros((rows, tok_count), F32)
-    gate = jnp.zeros((rows, tok_count), F32)
-    for k in range(top):
-        hit = routes_ref[k : k + 1, :] == expert
+    for hit in hits:
         named = jnp.where(hit, 1.0, named)
-        gate = jnp.where(hit, gates_ref[k : k + 1, :], gate)
     count = dot(named.astype(BF), earlier)
     here = (named > 0.0) & (count == (row % capacity).astype(F32))
+    return hits, here
+
+
+def dispatch_kernel(
+    capacity, quarter_ref, routes_hbm, gates_hbm, grad_hbm, slots_ref, routes_ref, gates_ref, cols_ref, sems
+):
+    rows, piece = slots_ref.shape
+    start = pl.multiple_of(quarter_ref[0] * piece, piece)
+    copies = [
+        pltpu.make_async_copy(routes_hbm, routes_ref, sems.at[0]),
+        pltpu.make_async_copy(gates_hbm, gates_ref, sems.at[1]),
+        pltpu.make_async_copy(grad_hbm.at[:, pl.ds(start, piece)], cols_ref, sems.at[2]),
+    ]
+    for copy in copies:
+        copy.start()
+    copies[0].wait()
+    hits, here = slot_hits(routes_ref[...], capacity, rows)
+    copies[1].wait()
+    gate = jnp.zeros(here.shape, F32)
+    for k, hit in enumerate(hits):
+        gate = jnp.where(hit, gates_ref[k : k + 1, :], gate)
     weight = jnp.sum(jnp.where(here, gate, 0.0), axis=1, keepdims=True)
-    pick = one_hot(here)
-    pick_ref[...] = pick
-    slots_ref[...] = (dot(pick, cols) * weight).astype(BF)
+    copies[2].wait()
+    slots_ref[...] = (dot(one_hot(here), cols_ref[...]) * weight).astype(BF)
+
+
+def pick_kernel(capacity, routes_ref, pick_ref):
+    tok_count, rows = pick_ref.shape
+    _, here = slot_hits(routes_ref[...], capacity, rows)
+    square = (tok_count, tok_count)
+    pick_ref[...] = dot_t(one_hot(iota(square, 0) == iota(square, 1)), one_hot(here)).astype(BF)
 
 
 def hidden_kernel(quarter_ref, rows_ref, *refs):
@@ -72,11 +95,10 @@
             out_ref[target, j * hidden : (j + 1) * hidden, :] = value.astype(BF)
 
 
-def expert_kernel(parts_ref, gate_ref, up_ref, wg_ref, wu_ref, out_ref):
-    quarters, groups, block, piece = out_ref.shape
+def expert_kernel(parts_ref, gate_ref, up_ref, wg_ref, wu_ref, out_hbm, out, sems):
+    quarters, groups, block, piece = out.shape
     experts_here, hidden, _ = wg_ref.shape
     capacity = block // experts_here
-    rows = groups * capacity
     grads = []
     for j in range(experts_here):
         band = slice(j * hidden, (j + 1) * hidden)
@@ -90,13 +112,18 @@
         d_gate = (d_hidden * up * (sig * (1.0 + act * (1.0 - sig)))).astype(BF)
         d_up = (d_hidden * (act * sig)).astype(BF)
         grads.append((d_gate, d_up))
+    copies = []
     for c in range(quarters):
         cols = slice(c * piece, (c + 1) * piece)
         values = []
         for j in range(experts_here):
             value = dot(grads[j][0], wg_ref[j, :, cols]) + dot(grads[j][1], wu_ref[j, :, cols])
             values.append(value.reshape(groups, capacity, piece))
-        out_ref[c] = jnp.concatenate(values, axis=1).astype(BF)
+        out[c] = jnp.concatenate(values, axis=1).astype(BF)
+        copies.append(pltpu.make_async_copy(out.at[c], out_hbm.at[c], sems.at[c]))
+        copies[-1].start()
+    for copy in copies:
+        copy.wait()
 
 
 def sum_kernel(parts_ref, out_ref):
@@ -108,12 +135,10 @@
 
 def combine_kernel(pick_ref, back_ref, out_ref):
     quarters, heads, packed, lanes = out_ref.shape
-    tok_count = pick_ref.shape[1]
+    tok_count = pick_ref.shape[0]
     part = tok_count // quarters
     tiles = packed // part
-    total = lax.dot_general(
-        pick_ref[...], back_ref[...], (((0,), (0,)), ((), ())), preferred_element_type=F32
-    ).astype(BF)
+    total = dot(pick_ref[...], back_ref[...]).astype(BF)
     to = iota((packed, tok_count), 0)
     token = iota((packed, tok_count), 1)
     for c in range(quarters):
@@ -137,7 +162,7 @@
 
 def finish_kernel(head_ref, moe_ref, pairs_ref, gain_ref, w_ref, resid_ref, grad_ref, moe):
     quarters, heads, packed, lanes = moe_ref.shape
-    part, width = resid_ref.shape
+    part, _, width = resid_ref.shape
     tiles = packed // part
     piece = tiles * lanes
     rows = heads * PAD
@@ -164,7 +189,7 @@
     mean = jnp.sum(scaled * normed, axis=1, keepdims=True) / width
     out_rows = dot(one_hot((item == first + part) & real), pairs)
     full = out_rows + inv_rms * (scaled - normed * mean)
-    resid_ref[...] = full[:part]
+    resid_ref[...] = full[:part].reshape(part, 1, width)
     product = dot_t(full.astype(BF), w_ref[...]).astype(BF)
     want = iota((heads * part, rows), 0)
     have = iota((heads * part, rows), 1)
@@ -172,15 +197,15 @@
     grad_ref[...] = dot(keep, product).astype(BF)
 
 
-def call(kernel, out_shape, specs, flops, moved, scratch=()):
+def call(kernel, out_shape, specs, flops, moved, scratch=(), out_specs=None, grant=GRANT):
     return pl.pallas_call(
         kernel,
         out_shape=out_shape,
         in_specs=specs,
-        out_specs=jax.tree.map(lambda _: VM, out_shape),
+        out_specs=out_specs or jax.tree.map(lambda _: VM, out_shape),
         scratch_shapes=scratch,
         cost_estimate=pl.CostEstimate(flops=flops, bytes_accessed=moved, transcendentals=0),
-        compiler_params=pltpu.CompilerParams(vmem_limit_bytes=GRANT),
+        compiler_params=pltpu.CompilerParams(vmem_limit_bytes=grant),
     )
 
 
@@ -208,12 +233,19 @@
     quarter = lax.axis_index("seq").astype(I32).reshape(1)
     head = lax.axis_index("head").astype(I32).reshape(1)
 
-    slots, pick = call(
+    slots = call(
         functools.partial(dispatch_kernel, capacity),
-        [sds((rows, piece), BF), sds((rows, tok_count), BF)],
-        [SM, VM, VM, VM],
+        sds((rows, piece), BF),
+        [SM, HB, HB, HB],
         2 * rows * tok_count * piece,
         1 << 20,
+        [
+            pltpu.VMEM(routes.T.shape, I32),
+            pltpu.VMEM(gates.T.shape, F32),
+            pltpu.VMEM((tok_count, piece), BF),
+            DMA((3,)),
+        ],
+        grant=None,
     )(quarter, routes.T, gates.T, out_grad)
 
     received = exchange(slots.reshape(exp_groups, block, piece), "exp")
@@ -250,6 +282,8 @@
         [VM] * 5,
         4 * rows * hidden * width,
         6 << 20,
+        [pltpu.VMEM((quarters, exp_groups, block, piece), BF), DMA((quarters,))],
+        HB,
     )(
         summands,
         gate_pre.reshape(experts_here, exp_groups * capacity, hidden),
@@ -269,7 +303,15 @@
     while step > 0:
         pairs = doubled(pairs, step)
         step //= 2
-    back, pairs = lax.optimization_barrier((back, pairs))
+    late_routes, summed = lax.optimization_barrier((routes.T, summed))
+    pick = call(
+        functools.partial(pick_kernel, capacity),
+        sds((tok_count, rows), BF),
+        [VM],
+        2 * rows * tok_count * tok_count,
+        1 << 19,
+    )(late_routes)
+    back, pick, pairs = lax.optimization_barrier((back, pick, pairs))
     combined = call(
         combine_kernel,
         sds((quarters, heads, packed, LANES), BF),
@@ -280,13 +322,19 @@
     got = exchange(combined.reshape(quarters * heads, packed, LANES), ("seq", "head"))
     resid, head_grad = call(
         finish_kernel,
-        [sds((part, width), F32), sds((heads * part, attn), BF)],
+        [sds((part, 1, width), F32), sds((heads * part, attn), BF)],
         [SM] + [VM] * 4,
         2 * heads * PAD * width * attn,
         4 << 20,
         [pltpu.VMEM((heads * PAD, width), F32)],
-    )(head, got.reshape(quarters, heads, packed, LANES), pairs, norm_gain[None, :], w_out)
-    return resid[None], head_grad[None]
+    )(
+        head,
+        got.reshape(quarters, heads, packed, LANES),
+        pairs,
+        norm_gain[None, :],
+        w_out,
+    )
+    return jnp.swapaxes(resid, 0, 1), head_grad[None]
 
 
 def solution(mesh):

time: 179 us -> 175 us (0.978)
  local copies, waits for them, and re-layouts: 8.02 us -> 3.81 us
    unnamed x33 -> x24, local copies, waits for them, and re-layouts: 5.54 us -> 1.8 us
    pallas_call x2 -> x3, Pallas kernels: 4.04 us -> 5.67 us  [the longest x1 2.64 us: shards(): call(functools.partial(dispatch_kernel, capacity), sds((rows, piece), BF)...]
  transfers between devices with their start and end apart: 10 -> 10, of which waited for: 7 -> 8; matrix products, arithmetic and copies ran while one was open for 2% -> 3% of each run, Pallas kernels for 0% -> 0%
where the time goes in v2:
time: 175 us
  waiting for transfers between devices  77.1 us (44%)
  starting transfers between devices  61.6 us (35%)
  blocking collectives  16.6 us (9%)
  Pallas kernels  12 us (7%)
  local copies, waits for them, and re-layouts  3.81 us (2%)
  other arithmetic  2.56 us (1%)
    all_to_all x4, waiting for transfers between devices, exchange(): return lax.all_to_all(blocks, axis, split_axis=0, concat_axis=0, tiled=True)  54 us
    all_to_all x4, starting transfers between devices, exchange(): return lax.all_to_all(blocks, axis, split_axis=0, concat_axis=0, tiled=True)  36.6 us
    ppermute x3, waiting for transfers between devices, doubled(): other = lax.ppermute(values, 'head', [(i, i ^ step) for i in range(heads)])  23.1 us
    all_to_all x1, blocking collectives, exchange(): return lax.all_to_all(blocks, axis, split_axis=0, concat_axis=0, tiled=True)  16.6 us
    ppermute x3, starting transfers between devices, doubled(): other = lax.ppermute(values, 'head', [(i, i ^ step) for i in range(heads)])  13.6 us
    ppermute x3, starting transfers between devices, shards(): downs.append(lax.ppermute(own, 'seq', ring) if d else own)  11.4 us
  transfers between devices with their start and end apart: 10, of which 8 were waited for; matrix products, arithmetic and copies ran while one was open for 3% of the time, Pallas kernels for 0%

profile of v2, /device:TPU:8, one launch (start us, length us, event | category | flops | bytes accessed | tf_op | source)
XLA Modules:
  0.0 174.6 jit_solution(3916438884583120170)
XLA Ops:
  0.7 2.6 %shard_map.122 = bf16[512,512]{1,0:T(8,128)(2,1)} custom-call(s32[1]{0:T(128)} %bitcast.1.quarter_ref, s32[8,48]{1,0:T(8,128)} %bitcast.20, f32[8,48]{1,0:T(8,128)} %bitcast.24, bf16[48,2048]{1,0:T(8,128)(2,1)} %grad_hbm.1), custom_call_target="tpu_custom_call" | custom-call | flops 25165824 | bytes 1048576 | tf_op jit(solution)/shard_map/pallas_call | solution.py:236
  3.3 19.2 %all-to-all-start = ((bf16[32,16,512]{2,1,0:T(8,128)(2,1)}), bf16[32,16,512]{2,1,0:T(8,128)(2,1)S(1)}, u32[]{:S(2)}, u32[]{:S(2)}) async-start(bf16[32,16,512]{2,1,0:T(8,128)(2,1)} %bitcast.23), calls=%async_computation | async-start | bytes 1048576 | tf_op jit(solution)/shard_map/all_to_all | solution.py:213
  22.5 1.1 constant_dynamic-slice_fusion.2
  23.6 3.4 %collective-permute-start = (bf16[2,192,512]{2,1,0:T(8,128)(2,1)}, bf16[2,192,512]{2,1,0:T(8,128)(2,1)S(1)}, u32[]{:S(2)}, u32[]{:S(2)}) collective-permute-start(bf16[2,192,512]{2,1,0:T(8,128)(2,1)} %get-tuple-element.29), channel_id=1, source_target_pairs={{0,256},{256,512},{512,768},{768,0},{1,257},{257,513},{513,769},{7... | collective-permute-start | bytes 1179656 | tf_op jit(solution)/shard_map/ppermute | solution.py:258
  27.0 4.6 %collective-permute-start.1 = (bf16[2,192,512]{2,1,0:T(8,128)(2,1)}, bf16[2,192,512]{2,1,0:T(8,128)(2,1)S(1)}, u32[]{:S(2)}, u32[]{:S(2)}) collective-permute-start(bf16[2,192,512]{2,1,0:T(8,128)(2,1)} %get-tuple-element.31), channel_id=1, source_target_pairs={{0,512},{256,768},{512,0},{768,256},{1,513},{257,769},{513,1},{769... | collective-permute-start | bytes 1179656 | tf_op jit(solution)/shard_map/ppermute | solution.py:258
  31.6 3.3 %collective-permute-start.2 = (bf16[2,192,512]{2,1,0:T(8,128)(2,1)}, bf16[2,192,512]{2,1,0:T(8,128)(2,1)S(1)}, u32[]{:S(2)}, u32[]{:S(2)}) collective-permute-start(bf16[2,192,512]{2,1,0:T(8,128)(2,1)} %get-tuple-element.28), channel_id=1, source_target_pairs={{0,768},{256,0},{512,256},{768,512},{1,769},{257,1},{513,257},{769... | collective-permute-start | bytes 1179656 | tf_op jit(solution)/shard_map/ppermute | solution.py:258
  36.0 6.8 %collective-permute-start.3 = (bf16[24,2048]{1,0:T(8,128)(2,1)S(1)}, bf16[24,2048]{1,0:T(8,128)(2,1)S(1)}, u32[]{:S(2)}, u32[]{:S(2)}) collective-permute-start(bf16[24,2048]{1,0:T(8,128)(2,1)S(1)} %pad_maximum_fusion.3), channel_id=1, source_target_pairs={{0,4},{1,5},{2,6},{3,7},{4,0},{5,1},{6,2},{7,3},{8,12},{9,13},{10,... | collective-permute-start | bytes 294920 | tf_op jit(solution)/shard_map/ppermute | solution.py:264
  42.8 5.5 %collective-permute-done.3 = bf16[24,2048]{1,0:T(8,128)(2,1)S(1)} collective-permute-done((bf16[24,2048]{1,0:T(8,128)(2,1)S(1)}, bf16[24,2048]{1,0:T(8,128)(2,1)S(1)}, u32[]{:S(2)}, u32[]{:S(2)}) %collective-permute-start.3) | collective-permute-done | bytes 98336 | tf_op jit(solution)/shard_map/ppermute | solution.py:264
  49.9 6.4 %all-to-all-done.rows_ref = bf16[32,16,512]{2,1,0:T(8,128)(2,1)S(1)} async-done(((bf16[32,16,512]{2,1,0:T(8,128)(2,1)}), bf16[32,16,512]{2,1,0:T(8,128)(2,1)S(1)}, u32[]{:S(2)}, u32[]{:S(2)}) %all-to-all-start) | async-done | bytes 524320 | tf_op jit(solution)/shard_map/all_to_all | solution.py:213
  58.1 16.6 %all_to_all.25.parts_ref = bf16[4,384,256]{2,1,0:T(8,128)(2,1)S(1)} all-to-all(bf16[4,384,256]{2,1,0:T(8,128)(2,1)S(1)} %shard_map.123), channel_id=1, replica_groups=mesh['seq'=4,'exp'=32,'head'=8] {'seq'}, dimensions={0} | all-to-all | bytes 1572864 | tf_op jit(solution)/shard_map/all_to_all | solution.py:213
  74.7 2.2 %shard_map.124 = bf16[4,32,16,512]{3,2,1,0:T(8,128)(2,1)} custom-call(bf16[4,384,256]{2,1,0:T(8,128)(2,1)S(1)} %all_to_all.25.parts_ref, bf16[2,256,192]{2,1,0:T(8,128)(2,1)S(1)} %bitcast.18, bf16[2,256,192]{2,1,0:T(8,128)(2,1)S(1)} %bitcast.19, bf16[2,192,2048]{2,1,0:T(8,128)(2,1)S(1)} %bitcast.15, bf16[2,192,2048]{2,1,0:T(8,128)(2,1)S(1)} %bitcast.16), custom_call_target="tpu_custom_call" | custom-call | flops 805306368 | bytes 6291456 | tf_op jit(solution)/shard_map/pallas_call | solution.py:279
  76.9 3.8 %all-to-all-start.2 = ((bf16[4,32,16,512]{3,2,1,0:T(8,128)(2,1)}), bf16[4,32,16,512]{3,2,1,0:T(8,128)(2,1)S(1)}, u32[]{:S(2)}, u32[]{:S(2)}) async-start(bf16[4,32,16,512]{3,2,1,0:T(8,128)(2,1)} %shard_map.124), calls=%async_computation.2 | async-start | bytes 4194304 | tf_op jit(solution)/shard_map/all_to_all | solution.py:213
  80.7 4.5 %collective-permute-start.4 = (bf16[48,2048]{1,0:T(8,128)(2,1)S(1)}, bf16[48,2048]{1,0:T(8,128)(2,1)S(1)}, u32[]{:S(2)}, u32[]{:S(2)}) collective-permute-start(bf16[48,2048]{1,0:T(8,128)(2,1)S(1)} %copy-done.11), channel_id=1, source_target_pairs={{0,2},{1,3},{2,0},{3,1},{4,6},{5,7},{6,4},{7,5},{8,10},{9,11},{10,... | collective-permute-start | bytes 589832 | tf_op jit(solution)/shard_map/ppermute | solution.py:264
  85.2 7.0 %collective-permute-done.4 = bf16[48,2048]{1,0:T(8,128)(2,1)S(1)} collective-permute-done((bf16[48,2048]{1,0:T(8,128)(2,1)S(1)}, bf16[48,2048]{1,0:T(8,128)(2,1)S(1)}, u32[]{:S(2)}, u32[]{:S(2)}) %collective-permute-start.4) | collective-permute-done | bytes 196640 | tf_op jit(solution)/shard_map/ppermute | solution.py:264
  93.0 13.1 %all-to-all-done.2.parts_ref = bf16[4,32,16,512]{3,2,1,0:T(8,128)(2,1)S(1)} async-done(((bf16[4,32,16,512]{3,2,1,0:T(8,128)(2,1)}), bf16[4,32,16,512]{3,2,1,0:T(8,128)(2,1)S(1)}, u32[]{:S(2)}, u32[]{:S(2)}) %all-to-all-start.2) | async-done | bytes 2097184 | tf_op jit(solution)/shard_map/all_to_all | solution.py:213
  106.0 1.1 shard_map.125
  107.1 5.4 %all-to-all-start.3 = ((bf16[32,16,512]{2,1,0:T(8,128)(2,1)}), bf16[32,16,512]{2,1,0:T(8,128)(2,1)}, u32[]{:S(2)}, u32[]{:S(2)}) async-start(bf16[32,16,512]{2,1,0:T(8,128)(2,1)} %shard_map.125), calls=%async_computation.3 | async-start | bytes 1048576 | tf_op jit(solution)/shard_map/all_to_all | solution.py:213
  112.5 2.3 %collective-permute-start.5 = (bf16[96,2048]{1,0:T(8,128)(2,1)}, bf16[96,2048]{1,0:T(8,128)(2,1)S(1)}, u32[]{:S(2)}, u32[]{:S(2)}) collective-permute-start(bf16[96,2048]{1,0:T(8,128)(2,1)} %pad_maximum_fusion.1), channel_id=1, source_target_pairs={{0,1},{1,0},{2,3},{3,2},{4,5},{5,4},{6,7},{7,6},{8,9},{9,8},{10,11... | collective-permute-start | bytes 1179656 | tf_op jit(solution)/shard_map/ppermute | solution.py:264
  115.3 10.6 %collective-permute-done.5 = bf16[96,2048]{1,0:T(8,128)(2,1)S(1)} collective-permute-done((bf16[96,2048]{1,0:T(8,128)(2,1)}, bf16[96,2048]{1,0:T(8,128)(2,1)S(1)}, u32[]{:S(2)}, u32[]{:S(2)}) %collective-permute-start.5) | collective-permute-done | bytes 393248 | tf_op jit(solution)/shard_map/ppermute | solution.py:264
  126.9 19.4 %all-to-all-done.3 = bf16[32,16,512]{2,1,0:T(8,128)(2,1)} async-done(((bf16[32,16,512]{2,1,0:T(8,128)(2,1)}), bf16[32,16,512]{2,1,0:T(8,128)(2,1)}, u32[]{:S(2)}, u32[]{:S(2)}) %all-to-all-start.3) | async-done | bytes 524320 | tf_op jit(solution)/shard_map/all_to_all | solution.py:213
  146.3 2.2 %shard_map.127 = bf16[4,8,48,128]{3,2,1,0:T(8,128)(2,1)} custom-call(bf16[48,512]{1,0:T(8,128)(2,1)S(1)} %shard_map.126.pick_ref, bf16[512,512]{1,0:T(8,128)(2,1)} %bitcast.9.back_ref), custom_call_target="tpu_custom_call" | custom-call | flops 25165824 | bytes 1048576 | tf_op jit(solution)/shard_map/pallas_call | solution.py:315
  148.5 8.3 %all-to-all-start.4 = ((bf16[32,48,128]{2,1,0:T(8,128)(2,1)}), bf16[32,48,128]{2,1,0:T(8,128)(2,1)S(1)}, u32[]{:S(2)}, u32[]{:S(2)}) async-start(bf16[32,48,128]{2,1,0:T(8,128)(2,1)} %bitcast.10), calls=%async_computation.4 | async-start | bytes 786432 | tf_op jit(solution)/shard_map/all_to_all | solution.py:213
  156.8 15.2 %all-to-all-done.4 = bf16[32,48,128]{2,1,0:T(8,128)(2,1)S(1)} async-done(((bf16[32,48,128]{2,1,0:T(8,128)(2,1)}), bf16[32,48,128]{2,1,0:T(8,128)(2,1)S(1)}, u32[]{:S(2)}, u32[]{:S(2)}) %all-to-all-start.4) | async-done | bytes 393248 | tf_op jit(solution)/shard_map/all_to_all | solution.py:213
  172.0 2.6 %shard_map.128 = (f32[12,1,2048]{2,1,0:T(1,128)}, bf16[96,512]{1,0:T(8,128)(2,1)}) custom-call(s32[1]{0:T(128)} %bitcast.head_ref, bf16[4,8,48,128]{3,2,1,0:T(8,128)(2,1)S(1)} %bitcast.17, bf16[192,2048]{1,0:T(8,128)(2,1)S(1)} %pad_maximum_fusion.pairs_ref, f32[1,2048]{1,0:T(1,128)S(1)} %bitcast.22, bf16[512,2048]{1,0:T(8,128)(2,1)S(1)} %copy-done.1), custom_call_target="tpu_custom_call" | custom-call | flops 268435456 | bytes 4194304 | tf_op jit(solution)/shard_map/pallas_call | solution.py:323
  (35 shorter events, 6.6 us)
Async XLA Ops:
  0.6 35.3 %copy-start = (bf16[48,2048]{1,0:T(8,128)(2,1)S(1)}, bf16[48,2048]{1,0:T(8,128)(2,1)}, u32[]{:S(2)}) copy-start(bf16[48,2048]{1,0:T(8,128)(2,1)} %param.12) | copy-start | bytes 589828
  0.6 21.9 %copy-start.10 = (bf16[2,192,2048]{2,1,0:T(8,128)(2,1)S(1)}, bf16[2,192,2048]{2,1,0:T(8,128)(2,1)}, u32[]{:S(2)}) copy-start(bf16[2,192,2048]{2,1,0:T(8,128)(2,1)} %param.20) | copy-start | bytes 4718596
  3.3 53.0 %all-to-all-start = ((bf16[32,16,512]{2,1,0:T(8,128)(2,1)}), bf16[32,16,512]{2,1,0:T(8,128)(2,1)S(1)}, u32[]{:S(2)}, u32[]{:S(2)}) async-start(bf16[32,16,512]{2,1,0:T(8,128)(2,1)} %bitcast.23), calls=%async_computation | async-start | bytes 1048576 | tf_op jit(solution)/shard_map/all_to_all | solution.py:213
  23.6 25.5 %collective-permute-start = (bf16[2,192,512]{2,1,0:T(8,128)(2,1)}, bf16[2,192,512]{2,1,0:T(8,128)(2,1)S(1)}, u32[]{:S(2)}, u32[]{:S(2)}) collective-permute-start(bf16[2,192,512]{2,1,0:T(8,128)(2,1)} %get-tuple-element.29), channel_id=1, source_target_pairs={{0,256},{256,512},{512,768},{768,0},{1,257},{257,513},{513,769},{7... | collective-permute-start | bytes 1179656 | tf_op jit(solution)/shard_map/ppermute | solution.py:258
  27.0 22.1 %collective-permute-start.1 = (bf16[2,192,512]{2,1,0:T(8,128)(2,1)}, bf16[2,192,512]{2,1,0:T(8,128)(2,1)S(1)}, u32[]{:S(2)}, u32[]{:S(2)}) collective-permute-start(bf16[2,192,512]{2,1,0:T(8,128)(2,1)} %get-tuple-element.31), channel_id=1, source_target_pairs={{0,512},{256,768},{512,0},{768,256},{1,513},{257,769},{513,1},{769... | collective-permute-start | bytes 1179656 | tf_op jit(solution)/shard_map/ppermute | solution.py:258
  31.6 17.5 %collective-permute-start.2 = (bf16[2,192,512]{2,1,0:T(8,128)(2,1)}, bf16[2,192,512]{2,1,0:T(8,128)(2,1)S(1)}, u32[]{:S(2)}, u32[]{:S(2)}) collective-permute-start(bf16[2,192,512]{2,1,0:T(8,128)(2,1)} %get-tuple-element.28), channel_id=1, source_target_pairs={{0,768},{256,0},{512,256},{768,512},{1,769},{257,1},{513,257},{769... | collective-permute-start | bytes 1179656 | tf_op jit(solution)/shard_map/ppermute | solution.py:258
  36.0 12.4 %collective-permute-start.3 = (bf16[24,2048]{1,0:T(8,128)(2,1)S(1)}, bf16[24,2048]{1,0:T(8,128)(2,1)S(1)}, u32[]{:S(2)}, u32[]{:S(2)}) collective-permute-start(bf16[24,2048]{1,0:T(8,128)(2,1)S(1)} %pad_maximum_fusion.3), channel_id=1, source_target_pairs={{0,4},{1,5},{2,6},{3,7},{4,0},{5,1},{6,2},{7,3},{8,12},{9,13},{10,... | collective-permute-start | bytes 294920 | tf_op jit(solution)/shard_map/ppermute | solution.py:264
  49.1 0.8 copy-start.4
  49.9 24.8 %copy-start.2 = (bf16[2,2048,192]{1,2,0:T(8,128)(2,1)S(1)}, bf16[2,2048,192]{1,2,0:T(8,128)(2,1)}, u32[]{:S(2)}) copy-start(bf16[2,2048,192]{1,2,0:T(8,128)(2,1)} %param.18) | copy-start | bytes 4718596
  56.3 1.0 copy-start.5
  57.3 17.4 %copy-start.3 = (bf16[2,2048,192]{1,2,0:T(8,128)(2,1)S(1)}, bf16[2,2048,192]{1,2,0:T(8,128)(2,1)}, u32[]{:S(2)}) copy-start(bf16[2,2048,192]{1,2,0:T(8,128)(2,1)} %param.19) | copy-start | bytes 4718596
  57.3 17.4 %copy-start.6 = (bf16[1,2,32,8,192]{4,3,2,1,0:T(8,128)(2,1)S(1)}, bf16[1,2,32,8,192]{4,3,2,1,0:T(8,128)(2,1)}, u32[]{:S(2)}) copy-start(bf16[1,2,32,8,192]{4,3,2,1,0:T(8,128)(2,1)} %param.16) | copy-start | bytes 589828
  57.3 17.4 %copy-start.7 = (bf16[1,2,32,8,192]{4,3,2,1,0:T(8,128)(2,1)S(1)}, bf16[1,2,32,8,192]{4,3,2,1,0:T(8,128)(2,1)}, u32[]{:S(2)}) copy-start(bf16[1,2,32,8,192]{4,3,2,1,0:T(8,128)(2,1)} %param.17) | copy-start | bytes 589828
  76.9 3.8 %copy-start.11 = (bf16[48,2048]{1,0:T(8,128)(2,1)S(1)}, bf16[48,2048]{1,0:T(8,128)(2,1)}, u32[]{:S(2)}) copy-start(bf16[48,2048]{1,0:T(8,128)(2,1)} %pad_maximum_fusion.2) | copy-start | bytes 589828
  76.9 29.1 %all-to-all-start.2 = ((bf16[4,32,16,512]{3,2,1,0:T(8,128)(2,1)}), bf16[4,32,16,512]{3,2,1,0:T(8,128)(2,1)S(1)}, u32[]{:S(2)}, u32[]{:S(2)}) async-start(bf16[4,32,16,512]{3,2,1,0:T(8,128)(2,1)} %shard_map.124), calls=%async_computation.2 | async-start | bytes 4194304 | tf_op jit(solution)/shard_map/all_to_all | solution.py:213
  80.7 11.5 %collective-permute-start.4 = (bf16[48,2048]{1,0:T(8,128)(2,1)S(1)}, bf16[48,2048]{1,0:T(8,128)(2,1)S(1)}, u32[]{:S(2)}, u32[]{:S(2)}) collective-permute-start(bf16[48,2048]{1,0:T(8,128)(2,1)S(1)} %copy-done.11), channel_id=1, source_target_pairs={{0,2},{1,3},{2,0},{3,1},{4,6},{5,7},{6,4},{7,5},{8,10},{9,11},{10,... | collective-permute-start | bytes 589832 | tf_op jit(solution)/shard_map/ppermute | solution.py:264
  93.0 21.9 %copy-start.8 = (s32[48,8]{0,1:T(8,128)S(1)}, s32[48,8]{0,1:T(8,128)}, u32[]{:S(2)}) copy-start(s32[48,8]{0,1:T(8,128)} %param.14) | copy-start | bytes 4612
  107.1 39.2 %all-to-all-start.3 = ((bf16[32,16,512]{2,1,0:T(8,128)(2,1)}), bf16[32,16,512]{2,1,0:T(8,128)(2,1)}, u32[]{:S(2)}, u32[]{:S(2)}) async-start(bf16[32,16,512]{2,1,0:T(8,128)(2,1)} %shard_map.125), calls=%async_computation.3 | async-start | bytes 1048576 | tf_op jit(solution)/shard_map/all_to_all | solution.py:213
  112.5 13.3 %collective-permute-start.5 = (bf16[96,2048]{1,0:T(8,128)(2,1)}, bf16[96,2048]{1,0:T(8,128)(2,1)S(1)}, u32[]{:S(2)}, u32[]{:S(2)}) collective-permute-start(bf16[96,2048]{1,0:T(8,128)(2,1)} %pad_maximum_fusion.1), channel_id=1, source_target_pairs={{0,1},{1,0},{2,3},{3,2},{4,5},{5,4},{6,7},{7,6},{8,9},{9,8},{10,11... | collective-permute-start | bytes 1179656 | tf_op jit(solution)/shard_map/ppermute | solution.py:264
  115.3 56.7 %copy-start.1 = (bf16[512,2048]{1,0:T(8,128)(2,1)S(1)}, bf16[512,2048]{1,0:T(8,128)(2,1)}, u32[]{:S(2)}) copy-start(bf16[512,2048]{1,0:T(8,128)(2,1)} %w_ref.1) | copy-start | bytes 6291460
  115.3 56.7 %copy-start.9 = (f32[2048]{0:T(1024)S(1)}, f32[2048]{0:T(1024)}, u32[]{:S(2)}) copy-start(f32[2048]{0:T(1024)} %param.13) | copy-start | bytes 24580
  148.5 23.5 %all-to-all-start.4 = ((bf16[32,48,128]{2,1,0:T(8,128)(2,1)}), bf16[32,48,128]{2,1,0:T(8,128)(2,1)S(1)}, u32[]{:S(2)}, u32[]{:S(2)}) async-start(bf16[32,48,128]{2,1,0:T(8,128)(2,1)} %bitcast.10), calls=%async_computation.4 | async-start | bytes 786432 | tf_op jit(solution)/shard_map/all_to_all | solution.py:213

commit v3 on v2

--- a/solution.py
+++ b/solution.py
@@ -35,11 +35,11 @@
     return lax.dot_general(a, b, (((1,), (1,)), ((), ())), preferred_element_type=F32)
 
 
-def slot_hits(routes, capacity, rows):
+def slot_hits(routes, capacity, rows, base=0):
     top, tok_count = routes.shape
     square = (tok_count, tok_count)
     earlier = one_hot(iota(square, 0) < iota(square, 1))
-    row = iota((rows, tok_count), 0)
+    row = base + iota((rows, tok_count), 0)
     hits = [routes[k : k + 1, :] == row // capacity for k in range(top)]
     named = jnp.zeros((rows, tok_count), F32)
     for hit in hits:
@@ -50,9 +50,9 @@
 
 
 def dispatch_kernel(
-    capacity, quarter_ref, routes_hbm, gates_hbm, grad_hbm, slots_ref, routes_ref, gates_ref, cols_ref, sems
+    capacity, quarter_ref, routes_hbm, gates_hbm, grad_hbm, slots_hbm, routes_ref, gates_ref, cols_ref, slots_ref, sems
 ):
-    rows, piece = slots_ref.shape
+    chunks, rows, piece = slots_ref.shape
     start = pl.multiple_of(quarter_ref[0] * piece, piece)
     copies = [
         pltpu.make_async_copy(routes_hbm, routes_ref, sems.at[0]),
@@ -61,15 +61,20 @@
     ]
     for copy in copies:
         copy.start()
-    copies[0].wait()
-    hits, here = slot_hits(routes_ref[...], capacity, rows)
-    copies[1].wait()
-    gate = jnp.zeros(here.shape, F32)
-    for k, hit in enumerate(hits):
-        gate = jnp.where(hit, gates_ref[k : k + 1, :], gate)
-    weight = jnp.sum(jnp.where(here, gate, 0.0), axis=1, keepdims=True)
-    copies[2].wait()
-    slots_ref[...] = (dot(one_hot(here), cols_ref[...]) * weight).astype(BF)
+    for copy in copies:
+        copy.wait()
+    outs = []
+    for c in range(chunks):
+        hits, here = slot_hits(routes_ref[...], capacity, rows, c * rows)
+        gate = jnp.zeros(here.shape, F32)
+        for k, hit in enumerate(hits):
+            gate = jnp.where(hit, gates_ref[k : k + 1, :], gate)
+        weight = jnp.sum(jnp.where(here, gate, 0.0), axis=1, keepdims=True)
+        slots_ref[c] = (dot(one_hot(here), cols_ref[...]) * weight).astype(BF)
+        outs.append(pltpu.make_async_copy(slots_ref.at[c], slots_hbm.at[c], sems.at[3 + c]))
+        outs[-1].start()
+    for copy in outs:
+        copy.wait()
 
 
 def pick_kernel(capacity, routes_ref, pick_ref):
@@ -126,11 +131,19 @@
         copy.wait()
 
 
-def sum_kernel(parts_ref, out_ref):
-    total = parts_ref[0].astype(F32)
-    for c in range(1, parts_ref.shape[0]):
-        total = total + parts_ref[c].astype(F32)
-    out_ref[...] = total.astype(BF)
+def sum_kernel(parts_ref, out_hbm, out, sems):
+    chunks = max(1, out.shape[0] // 8)
+    copies = []
+    for n in range(out.shape[0] // chunks):
+        some = slice(n * chunks, (n + 1) * chunks)
+        total = parts_ref[0, some].astype(F32)
+        for c in range(1, parts_ref.shape[0]):
+            total = total + parts_ref[c, some].astype(F32)
+        out[some] = total.astype(BF)
+        copies.append(pltpu.make_async_copy(out.at[some], out_hbm.at[some], sems.at[n]))
+        copies[-1].start()
+    for copy in copies:
+        copy.wait()
 
 
 def combine_kernel(pick_ref, back_ref, out_ref):
@@ -139,16 +152,16 @@
     part = tok_count // quarters
     tiles = packed // part
     total = dot(pick_ref[...], back_ref[...]).astype(BF)
-    to = iota((packed, tok_count), 0)
-    token = iota((packed, tok_count), 1)
+    stacked = jnp.concatenate([total[:, n * lanes : (n + 1) * lanes] for n in range(tiles)], axis=0)
+    size = quarters * packed
+    to = iota((size, size), 0)
+    have = iota((size, size), 1)
+    token = to // packed * part + to % part
+    tile = to % packed // part
+    value = dot(one_hot(have == tile * tok_count + token), stacked).astype(BF)
     for c in range(quarters):
-        value = jnp.zeros((packed, lanes), F32)
-        for n in range(tiles):
-            move = one_hot((to // part == n) & (c * part + to % part == token))
-            value = value + dot(move, total[:, n * lanes : (n + 1) * lanes])
-        value = value.astype(BF)
         for h in range(heads):
-            out_ref[c, h] = value
+            out_ref[c, h] = value[c * packed : (c + 1) * packed]
 
 
 def offset(index, heads):
@@ -173,21 +186,20 @@
     for n in range(tiles):
         want = source * packed + n * part + row % PAD
         move = one_hot((want == item) & (row % PAD < part))
+        blocks = [moe_ref[c].reshape(heads * packed, lanes) for c in range(quarters)]
+        moved = dot(move, jnp.concatenate(blocks, axis=1))
         for c in range(quarters):
-            block = moe_ref[c].reshape(heads * packed, lanes)
             start = c * piece + n * lanes
-            moe[:, start : start + lanes] = dot(move, block)
-    row = iota((rows, heads * 2 * part), 0)
-    item = iota((rows, heads * 2 * part), 1)
-    first = (row // PAD) * (2 * part) + row % PAD
-    real = row % PAD < part
-    pairs = pairs_ref[...]
-    x = dot(one_hot((item == first) & real), pairs)
+            moe[:, start : start + lanes] = moved[:, c * lanes : (c + 1) * lanes]
+    both = pairs_ref[...].astype(F32).reshape(heads, 2 * part, width)
+    x = both[:, :PAD].reshape(rows, width)
+    tail = both[:, 8:PAD].reshape(heads * 8, width)
+    tail = pltpu.roll(tail, heads * 8 - (PAD - part), 0).reshape(heads, 8, width)
+    out_rows = jnp.concatenate([both[:, PAD:], tail], axis=1).reshape(rows, width)
     inv_rms = lax.rsqrt(jnp.sum(x * x, axis=1, keepdims=True) / width + 1e-06)
     normed = x * inv_rms
     scaled = moe[...] * gain_ref[...]
     mean = jnp.sum(scaled * normed, axis=1, keepdims=True) / width
-    out_rows = dot(one_hot((item == first + part) & real), pairs)
     full = out_rows + inv_rms * (scaled - normed * mean)
     resid_ref[...] = full[:part].reshape(part, 1, width)
     product = dot_t(full.astype(BF), w_ref[...]).astype(BF)
@@ -233,9 +245,10 @@
     quarter = lax.axis_index("seq").astype(I32).reshape(1)
     head = lax.axis_index("head").astype(I32).reshape(1)
 
+    chunks = 4
     slots = call(
         functools.partial(dispatch_kernel, capacity),
-        sds((rows, piece), BF),
+        sds((chunks, rows // chunks, piece), BF),
         [SM, HB, HB, HB],
         2 * rows * tok_count * piece,
         1 << 20,
@@ -243,8 +256,10 @@
             pltpu.VMEM(routes.T.shape, I32),
             pltpu.VMEM(gates.T.shape, F32),
             pltpu.VMEM((tok_count, piece), BF),
-            DMA((3,)),
+            pltpu.VMEM((chunks, rows // chunks, piece), BF),
+            DMA((3 + chunks,)),
         ],
+        HB,
         grant=None,
     )(quarter, routes.T, gates.T, out_grad)
 
@@ -264,7 +279,8 @@
         other = lax.ppermute(values, "head", [(i, i ^ step) for i in range(heads)])
         return jnp.concatenate([values, other], axis=0)
 
-    pairs = jnp.concatenate([own_rows(layer_input), own_rows(out_grad)], axis=0)
+    own_grad = own_rows(out_grad)
+    pairs = jnp.concatenate([own_rows(layer_input), own_grad[8:], own_grad[:8]], axis=0)
     pairs = doubled(pairs, heads // 2)
     downs, pairs = lax.optimization_barrier((downs, pairs))
 
@@ -296,7 +312,13 @@
         pairs = doubled(pairs, heads // 4)
     mine, pairs = lax.optimization_barrier((mine, pairs))
     summed = call(
-        sum_kernel, sds((exp_groups, block, piece), BF), [VM], 4 * rows * piece, 3 << 20
+        sum_kernel,
+        sds((exp_groups, block, piece), BF),
+        [VM],
+        4 * rows * piece,
+        3 << 20,
+        [pltpu.VMEM((exp_groups, block, piece), BF), DMA((exp_groups // max(1, exp_groups // 8),))],
+        HB,
     )(mine)
     back = exchange(summed, "exp")
     step = heads // 8

time: 175 us -> 175 us (level)
  transfers between devices with their start and end apart: 10 -> 10, of which waited for: 8 -> 7; matrix products, arithmetic and copies ran while one was open for 3% -> 3% of each run, Pallas kernels for 0% -> 0%
where the time goes in v3:
time: 175 us; the launch traced here: 174 us
  waiting for transfers between devices  76.3 us (44%)
  starting transfers between devices  61.7 us (35%)
  blocking collectives  16.6 us (9%)
  Pallas kernels  11.5 us (7%)
  local copies, waits for them, and re-layouts  4.52 us (3%)
  other arithmetic  2.56 us (1%)
    all_to_all x4, waiting for transfers between devices, exchange(): return lax.all_to_all(blocks, axis, split_axis=0, concat_axis=0, tiled=True)  53.3 us
    all_to_all x4, starting transfers between devices, exchange(): return lax.all_to_all(blocks, axis, split_axis=0, concat_axis=0, tiled=True)  36.6 us
    ppermute x3, waiting for transfers between devices, doubled(): other = lax.ppermute(values, 'head', [(i, i ^ step) for i in range(heads)])  23 us
    all_to_all x1, blocking collectives, exchange(): return lax.all_to_all(blocks, axis, split_axis=0, concat_axis=0, tiled=True)  16.6 us
    ppermute x3, starting transfers between devices, doubled(): other = lax.ppermute(values, 'head', [(i, i ^ step) for i in range(heads)])  13.7 us
    ppermute x3, starting transfers between devices, shards(): downs.append(lax.ppermute(own, 'seq', ring) if d else own)  11.4 us
  transfers between devices with their start and end apart: 10, of which 7 were waited for; matrix products, arithmetic and copies ran while one was open for 3% of the time, Pallas kernels for 0%

profile of v3, /device:TPU:8, one launch (start us, length us, event | category | flops | bytes accessed | tf_op | source)
XLA Modules:
  0.0 174.1 jit_solution(15814075321748683476)
XLA Ops:
  0.7 2.6 %shard_map.122 = bf16[4,128,512]{2,1,0:T(8,128)(2,1)} custom-call(s32[1]{0:T(128)} %bitcast.1.quarter_ref, s32[8,48]{1,0:T(8,128)} %bitcast.20, f32[8,48]{1,0:T(8,128)} %bitcast.24, bf16[48,2048]{1,0:T(8,128)(2,1)} %grad_hbm.1), custom_call_target="tpu_custom_call" | custom-call | flops 25165824 | bytes 1048576 | tf_op jit(solution)/shard_map/pallas_call | solution.py:249
  3.2 19.2 %all-to-all-start = ((bf16[32,16,512]{2,1,0:T(8,128)(2,1)}), bf16[32,16,512]{2,1,0:T(8,128)(2,1)S(1)}, u32[]{:S(2)}, u32[]{:S(2)}) async-start(bf16[32,16,512]{2,1,0:T(8,128)(2,1)} %bitcast.23), calls=%async_computation | async-start | bytes 1048576 | tf_op jit(solution)/shard_map/all_to_all | solution.py:225
  22.4 1.1 constant_dynamic-slice_fusion.3
  23.5 3.4 %collective-permute-start = (bf16[2,192,512]{2,1,0:T(8,128)(2,1)}, bf16[2,192,512]{2,1,0:T(8,128)(2,1)S(1)}, u32[]{:S(2)}, u32[]{:S(2)}) collective-permute-start(bf16[2,192,512]{2,1,0:T(8,128)(2,1)} %get-tuple-element.29), channel_id=1, source_target_pairs={{0,256},{256,512},{512,768},{768,0},{1,257},{257,513},{513,769},{7... | collective-permute-start | bytes 1179656 | tf_op jit(solution)/shard_map/ppermute | solution.py:273
  26.9 4.6 %collective-permute-start.1 = (bf16[2,192,512]{2,1,0:T(8,128)(2,1)}, bf16[2,192,512]{2,1,0:T(8,128)(2,1)S(1)}, u32[]{:S(2)}, u32[]{:S(2)}) collective-permute-start(bf16[2,192,512]{2,1,0:T(8,128)(2,1)} %get-tuple-element.31), channel_id=1, source_target_pairs={{0,512},{256,768},{512,0},{768,256},{1,513},{257,769},{513,1},{769... | collective-permute-start | bytes 1179656 | tf_op jit(solution)/shard_map/ppermute | solution.py:273
  31.5 3.3 %collective-permute-start.2 = (bf16[2,192,512]{2,1,0:T(8,128)(2,1)}, bf16[2,192,512]{2,1,0:T(8,128)(2,1)S(1)}, u32[]{:S(2)}, u32[]{:S(2)}) collective-permute-start(bf16[2,192,512]{2,1,0:T(8,128)(2,1)} %get-tuple-element.28), channel_id=1, source_target_pairs={{0,768},{256,0},{512,256},{768,512},{1,769},{257,1},{513,257},{769... | collective-permute-start | bytes 1179656 | tf_op jit(solution)/shard_map/ppermute | solution.py:273
  36.6 6.8 %collective-permute-start.3 = (bf16[24,2048]{1,0:T(8,128)(2,1)S(1)}, bf16[24,2048]{1,0:T(8,128)(2,1)S(1)}, u32[]{:S(2)}, u32[]{:S(2)}) collective-permute-start(bf16[24,2048]{1,0:T(8,128)(2,1)S(1)} %pad_maximum_fusion.3), channel_id=1, source_target_pairs={{0,4},{1,5},{2,6},{3,7},{4,0},{5,1},{6,2},{7,3},{8,12},{9,13},{10,... | collective-permute-start | bytes 294920 | tf_op jit(solution)/shard_map/ppermute | solution.py:279
  43.5 5.5 %collective-permute-done.3 = bf16[24,2048]{1,0:T(8,128)(2,1)S(1)} collective-permute-done((bf16[24,2048]{1,0:T(8,128)(2,1)S(1)}, bf16[24,2048]{1,0:T(8,128)(2,1)S(1)}, u32[]{:S(2)}, u32[]{:S(2)}) %collective-permute-start.3) | collective-permute-done | bytes 98336 | tf_op jit(solution)/shard_map/ppermute | solution.py:279
  50.5 5.7 %all-to-all-done.rows_ref = bf16[32,16,512]{2,1,0:T(8,128)(2,1)S(1)} async-done(((bf16[32,16,512]{2,1,0:T(8,128)(2,1)}), bf16[32,16,512]{2,1,0:T(8,128)(2,1)S(1)}, u32[]{:S(2)}, u32[]{:S(2)}) %all-to-all-start) | async-done | bytes 524320 | tf_op jit(solution)/shard_map/all_to_all | solution.py:225
  58.0 16.6 %all_to_all.25.parts_ref = bf16[4,384,256]{2,1,0:T(8,128)(2,1)S(1)} all-to-all(bf16[4,384,256]{2,1,0:T(8,128)(2,1)S(1)} %shard_map.123), channel_id=1, replica_groups=mesh['seq'=4,'exp'=32,'head'=8] {'seq'}, dimensions={0} | all-to-all | bytes 1572864 | tf_op jit(solution)/shard_map/all_to_all | solution.py:225
  74.6 2.2 %shard_map.124 = bf16[4,32,16,512]{3,2,1,0:T(8,128)(2,1)} custom-call(bf16[4,384,256]{2,1,0:T(8,128)(2,1)S(1)} %all_to_all.25.parts_ref, bf16[2,256,192]{2,1,0:T(8,128)(2,1)S(1)} %bitcast.18, bf16[2,256,192]{2,1,0:T(8,128)(2,1)S(1)} %bitcast.19, bf16[2,192,2048]{2,1,0:T(8,128)(2,1)S(1)} %bitcast.15, bf16[2,192,2048]{2,1,0:T(8,128)(2,1)S(1)} %bitcast.16), custom_call_target="tpu_custom_call" | custom-call | flops 805306368 | bytes 6291456 | tf_op jit(solution)/shard_map/pallas_call | solution.py:295
  76.9 3.8 %all-to-all-start.2 = ((bf16[4,32,16,512]{3,2,1,0:T(8,128)(2,1)}), bf16[4,32,16,512]{3,2,1,0:T(8,128)(2,1)S(1)}, u32[]{:S(2)}, u32[]{:S(2)}) async-start(bf16[4,32,16,512]{3,2,1,0:T(8,128)(2,1)} %shard_map.124), calls=%async_computation.2 | async-start | bytes 4194304 | tf_op jit(solution)/shard_map/all_to_all | solution.py:225
  80.6 4.5 %collective-permute-start.4 = (bf16[48,2048]{1,0:T(8,128)(2,1)S(1)}, bf16[48,2048]{1,0:T(8,128)(2,1)S(1)}, u32[]{:S(2)}, u32[]{:S(2)}) collective-permute-start(bf16[48,2048]{1,0:T(8,128)(2,1)S(1)} %copy-done.11), channel_id=1, source_target_pairs={{0,2},{1,3},{2,0},{3,1},{4,6},{5,7},{6,4},{7,5},{8,10},{9,11},{10,... | collective-permute-start | bytes 589832 | tf_op jit(solution)/shard_map/ppermute | solution.py:279
  85.1 7.0 %collective-permute-done.4 = bf16[48,2048]{1,0:T(8,128)(2,1)S(1)} collective-permute-done((bf16[48,2048]{1,0:T(8,128)(2,1)S(1)}, bf16[48,2048]{1,0:T(8,128)(2,1)S(1)}, u32[]{:S(2)}, u32[]{:S(2)}) %collective-permute-start.4) | collective-permute-done | bytes 196640 | tf_op jit(solution)/shard_map/ppermute | solution.py:279
  92.9 13.0 %all-to-all-done.2.parts_ref = bf16[4,32,16,512]{3,2,1,0:T(8,128)(2,1)S(1)} async-done(((bf16[4,32,16,512]{3,2,1,0:T(8,128)(2,1)}), bf16[4,32,16,512]{3,2,1,0:T(8,128)(2,1)S(1)}, u32[]{:S(2)}, u32[]{:S(2)}) %all-to-all-start.2) | async-done | bytes 2097184 | tf_op jit(solution)/shard_map/all_to_all | solution.py:225
  106.9 5.4 %all-to-all-start.3 = ((bf16[32,16,512]{2,1,0:T(8,128)(2,1)}), bf16[32,16,512]{2,1,0:T(8,128)(2,1)}, u32[]{:S(2)}, u32[]{:S(2)}) async-start(bf16[32,16,512]{2,1,0:T(8,128)(2,1)} %shard_map.125), calls=%async_computation.3 | async-start | bytes 1048576 | tf_op jit(solution)/shard_map/all_to_all | solution.py:225
  112.3 2.4 %collective-permute-start.5 = (bf16[96,2048]{1,0:T(8,128)(2,1)}, bf16[96,2048]{1,0:T(8,128)(2,1)S(1)}, u32[]{:S(2)}, u32[]{:S(2)}) collective-permute-start(bf16[96,2048]{1,0:T(8,128)(2,1)} %pad_maximum_fusion.1), channel_id=1, source_target_pairs={{0,1},{1,0},{2,3},{3,2},{4,5},{5,4},{6,7},{7,6},{8,9},{9,8},{10,11... | collective-permute-start | bytes 1179656 | tf_op jit(solution)/shard_map/ppermute | solution.py:279
  115.1 10.5 %collective-permute-done.5 = bf16[96,2048]{1,0:T(8,128)(2,1)S(1)} collective-permute-done((bf16[96,2048]{1,0:T(8,128)(2,1)}, bf16[96,2048]{1,0:T(8,128)(2,1)S(1)}, u32[]{:S(2)}, u32[]{:S(2)}) %collective-permute-start.5) | collective-permute-done | bytes 393248 | tf_op jit(solution)/shard_map/ppermute | solution.py:279
  125.7 1.1 pad_maximum_fusion.pairs_ref
  126.7 19.4 %all-to-all-done.3 = bf16[32,16,512]{2,1,0:T(8,128)(2,1)} async-done(((bf16[32,16,512]{2,1,0:T(8,128)(2,1)}), bf16[32,16,512]{2,1,0:T(8,128)(2,1)}, u32[]{:S(2)}, u32[]{:S(2)}) %all-to-all-start.3) | async-done | bytes 524320 | tf_op jit(solution)/shard_map/all_to_all | solution.py:225
  146.1 2.2 %shard_map.127 = bf16[4,8,48,128]{3,2,1,0:T(8,128)(2,1)} custom-call(bf16[48,512]{1,0:T(8,128)(2,1)S(1)} %shard_map.126.pick_ref, bf16[512,512]{1,0:T(8,128)(2,1)} %bitcast.9.back_ref), custom_call_target="tpu_custom_call" | custom-call | flops 25165824 | bytes 1048576 | tf_op jit(solution)/shard_map/pallas_call | solution.py:337
  148.3 8.3 %all-to-all-start.4 = ((bf16[32,48,128]{2,1,0:T(8,128)(2,1)}), bf16[32,48,128]{2,1,0:T(8,128)(2,1)S(1)}, u32[]{:S(2)}, u32[]{:S(2)}) async-start(bf16[32,48,128]{2,1,0:T(8,128)(2,1)} %bitcast.10), calls=%async_computation.4 | async-start | bytes 786432 | tf_op jit(solution)/shard_map/all_to_all | solution.py:225
  156.7 15.2 %all-to-all-done.4 = bf16[32,48,128]{2,1,0:T(8,128)(2,1)S(1)} async-done(((bf16[32,48,128]{2,1,0:T(8,128)(2,1)}), bf16[32,48,128]{2,1,0:T(8,128)(2,1)S(1)}, u32[]{:S(2)}, u32[]{:S(2)}) %all-to-all-start.4) | async-done | bytes 393248 | tf_op jit(solution)/shard_map/all_to_all | solution.py:225
  171.8 2.3 %shard_map.128 = (f32[12,1,2048]{2,1,0:T(1,128)}, bf16[96,512]{1,0:T(8,128)(2,1)}) custom-call(s32[1]{0:T(128)} %bitcast.head_ref, bf16[4,8,48,128]{3,2,1,0:T(8,128)(2,1)S(1)} %bitcast.17, bf16[192,2048]{1,0:T(8,128)(2,1)S(1)} %pad_maximum_fusion.pairs_ref, f32[1,2048]{1,0:T(1,128)S(1)} %bitcast.22, bf16[512,2048]{1,0:T(8,128)(2,1)S(1)} %copy-done.1), custom_call_target="tpu_custom_call" | custom-call | flops 268435456 | bytes 4194304 | tf_op jit(solution)/shard_map/pallas_call | solution.py:345
  (36 shorter events, 7.1 us)
Async XLA Ops:
  0.6 35.9 %copy-start = (bf16[48,2048]{1,0:T(8,128)(2,1)S(1)}, bf16[48,2048]{1,0:T(8,128)(2,1)}, u32[]{:S(2)}) copy-start(bf16[48,2048]{1,0:T(8,128)(2,1)} %param.12) | copy-start | bytes 589828
  0.6 21.8 %copy-start.10 = (bf16[2,192,2048]{2,1,0:T(8,128)(2,1)S(1)}, bf16[2,192,2048]{2,1,0:T(8,128)(2,1)}, u32[]{:S(2)}) copy-start(bf16[2,192,2048]{2,1,0:T(8,128)(2,1)} %param.20) | copy-start | bytes 4718596
  3.2 53.0 %all-to-all-start = ((bf16[32,16,512]{2,1,0:T(8,128)(2,1)}), bf16[32,16,512]{2,1,0:T(8,128)(2,1)S(1)}, u32[]{:S(2)}, u32[]{:S(2)}) async-start(bf16[32,16,512]{2,1,0:T(8,128)(2,1)} %bitcast.23), calls=%async_computation | async-start | bytes 1048576 | tf_op jit(solution)/shard_map/all_to_all | solution.py:225
  23.5 26.2 %collective-permute-start = (bf16[2,192,512]{2,1,0:T(8,128)(2,1)}, bf16[2,192,512]{2,1,0:T(8,128)(2,1)S(1)}, u32[]{:S(2)}, u32[]{:S(2)}) collective-permute-start(bf16[2,192,512]{2,1,0:T(8,128)(2,1)} %get-tuple-element.29), channel_id=1, source_target_pairs={{0,256},{256,512},{512,768},{768,0},{1,257},{257,513},{513,769},{7... | collective-permute-start | bytes 1179656 | tf_op jit(solution)/shard_map/ppermute | solution.py:273
  26.9 22.8 %collective-permute-start.1 = (bf16[2,192,512]{2,1,0:T(8,128)(2,1)}, bf16[2,192,512]{2,1,0:T(8,128)(2,1)S(1)}, u32[]{:S(2)}, u32[]{:S(2)}) collective-permute-start(bf16[2,192,512]{2,1,0:T(8,128)(2,1)} %get-tuple-element.31), channel_id=1, source_target_pairs={{0,512},{256,768},{512,0},{768,256},{1,513},{257,769},{513,1},{769... | collective-permute-start | bytes 1179656 | tf_op jit(solution)/shard_map/ppermute | solution.py:273
  31.5 18.2 %collective-permute-start.2 = (bf16[2,192,512]{2,1,0:T(8,128)(2,1)}, bf16[2,192,512]{2,1,0:T(8,128)(2,1)S(1)}, u32[]{:S(2)}, u32[]{:S(2)}) collective-permute-start(bf16[2,192,512]{2,1,0:T(8,128)(2,1)} %get-tuple-element.28), channel_id=1, source_target_pairs={{0,768},{256,0},{512,256},{768,512},{1,769},{257,1},{513,257},{769... | collective-permute-start | bytes 1179656 | tf_op jit(solution)/shard_map/ppermute | solution.py:273
  36.6 12.4 %collective-permute-start.3 = (bf16[24,2048]{1,0:T(8,128)(2,1)S(1)}, bf16[24,2048]{1,0:T(8,128)(2,1)S(1)}, u32[]{:S(2)}, u32[]{:S(2)}) collective-permute-start(bf16[24,2048]{1,0:T(8,128)(2,1)S(1)} %pad_maximum_fusion.3), channel_id=1, source_target_pairs={{0,4},{1,5},{2,6},{3,7},{4,0},{5,1},{6,2},{7,3},{8,12},{9,13},{10,... | collective-permute-start | bytes 294920 | tf_op jit(solution)/shard_map/ppermute | solution.py:279
  49.7 0.8 copy-start.4
  50.5 24.1 %copy-start.2 = (bf16[2,2048,192]{1,2,0:T(8,128)(2,1)S(1)}, bf16[2,2048,192]{1,2,0:T(8,128)(2,1)}, u32[]{:S(2)}) copy-start(bf16[2,2048,192]{1,2,0:T(8,128)(2,1)} %param.18) | copy-start | bytes 4718596
  56.2 1.0 copy-start.5
  57.2 17.4 %copy-start.3 = (bf16[2,2048,192]{1,2,0:T(8,128)(2,1)S(1)}, bf16[2,2048,192]{1,2,0:T(8,128)(2,1)}, u32[]{:S(2)}) copy-start(bf16[2,2048,192]{1,2,0:T(8,128)(2,1)} %param.19) | copy-start | bytes 4718596
  57.2 17.4 %copy-start.6 = (bf16[1,2,32,8,192]{4,3,2,1,0:T(8,128)(2,1)S(1)}, bf16[1,2,32,8,192]{4,3,2,1,0:T(8,128)(2,1)}, u32[]{:S(2)}) copy-start(bf16[1,2,32,8,192]{4,3,2,1,0:T(8,128)(2,1)} %param.16) | copy-start | bytes 589828
  57.2 17.4 %copy-start.7 = (bf16[1,2,32,8,192]{4,3,2,1,0:T(8,128)(2,1)S(1)}, bf16[1,2,32,8,192]{4,3,2,1,0:T(8,128)(2,1)}, u32[]{:S(2)}) copy-start(bf16[1,2,32,8,192]{4,3,2,1,0:T(8,128)(2,1)} %param.17) | copy-start | bytes 589828
  76.8 3.8 %copy-start.11 = (bf16[48,2048]{1,0:T(8,128)(2,1)S(1)}, bf16[48,2048]{1,0:T(8,128)(2,1)}, u32[]{:S(2)}) copy-start(bf16[48,2048]{1,0:T(8,128)(2,1)} %pad_maximum_fusion.2) | copy-start | bytes 589828
  76.9 29.1 %all-to-all-start.2 = ((bf16[4,32,16,512]{3,2,1,0:T(8,128)(2,1)}), bf16[4,32,16,512]{3,2,1,0:T(8,128)(2,1)S(1)}, u32[]{:S(2)}, u32[]{:S(2)}) async-start(bf16[4,32,16,512]{3,2,1,0:T(8,128)(2,1)} %shard_map.124), calls=%async_computation.2 | async-start | bytes 4194304 | tf_op jit(solution)/shard_map/all_to_all | solution.py:225
  80.6 11.5 %collective-permute-start.4 = (bf16[48,2048]{1,0:T(8,128)(2,1)S(1)}, bf16[48,2048]{1,0:T(8,128)(2,1)S(1)}, u32[]{:S(2)}, u32[]{:S(2)}) collective-permute-start(bf16[48,2048]{1,0:T(8,128)(2,1)S(1)} %copy-done.11), channel_id=1, source_target_pairs={{0,2},{1,3},{2,0},{3,1},{4,6},{5,7},{6,4},{7,5},{8,10},{9,11},{10,... | collective-permute-start | bytes 589832 | tf_op jit(solution)/shard_map/ppermute | solution.py:279
  92.9 21.8 %copy-start.8 = (s32[48,8]{0,1:T(8,128)S(1)}, s32[48,8]{0,1:T(8,128)}, u32[]{:S(2)}) copy-start(s32[48,8]{0,1:T(8,128)} %param.14) | copy-start | bytes 4612
  106.9 39.2 %all-to-all-start.3 = ((bf16[32,16,512]{2,1,0:T(8,128)(2,1)}), bf16[32,16,512]{2,1,0:T(8,128)(2,1)}, u32[]{:S(2)}, u32[]{:S(2)}) async-start(bf16[32,16,512]{2,1,0:T(8,128)(2,1)} %shard_map.125), calls=%async_computation.3 | async-start | bytes 1048576 | tf_op jit(solution)/shard_map/all_to_all | solution.py:225
  112.3 13.3 %collective-permute-start.5 = (bf16[96,2048]{1,0:T(8,128)(2,1)}, bf16[96,2048]{1,0:T(8,128)(2,1)S(1)}, u32[]{:S(2)}, u32[]{:S(2)}) collective-permute-start(bf16[96,2048]{1,0:T(8,128)(2,1)} %pad_maximum_fusion.1), channel_id=1, source_target_pairs={{0,1},{1,0},{2,3},{3,2},{4,5},{5,4},{6,7},{7,6},{8,9},{9,8},{10,11... | collective-permute-start | bytes 1179656 | tf_op jit(solution)/shard_map/ppermute | solution.py:279
  115.1 56.7 %copy-start.1 = (bf16[512,2048]{1,0:T(8,128)(2,1)S(1)}, bf16[512,2048]{1,0:T(8,128)(2,1)}, u32[]{:S(2)}) copy-start(bf16[512,2048]{1,0:T(8,128)(2,1)} %w_ref.1) | copy-start | bytes 6291460
  115.1 56.7 %copy-start.9 = (f32[2048]{0:T(1024)S(1)}, f32[2048]{0:T(1024)}, u32[]{:S(2)}) copy-start(f32[2048]{0:T(1024)} %param.13) | copy-start | bytes 24580
  148.3 23.5 %all-to-all-start.4 = ((bf16[32,48,128]{2,1,0:T(8,128)(2,1)}), bf16[32,48,128]{2,1,0:T(8,128)(2,1)S(1)}, u32[]{:S(2)}, u32[]{:S(2)}) async-start(bf16[32,48,128]{2,1,0:T(8,128)(2,1)} %bitcast.10), calls=%async_computation.4 | async-start | bytes 786432 | tf_op jit(solution)/shard_map/all_to_all | solution.py:225

commit v4 on v3

--- a/solution.py
+++ b/solution.py
@@ -90,13 +90,14 @@
     experts_here, hidden, _ = downs[0].shape
     capacity = block // experts_here
     quarters = len(downs)
+    own = pl.ds(pl.multiple_of(quarter_ref[0] * piece, piece), piece)
     wide = rows_ref[...].astype(F32)
     for j in range(experts_here):
         mine = wide[:, j * capacity : (j + 1) * capacity, :]
         mine = mine.reshape(groups * capacity, piece).astype(BF)
         for d in range(quarters):
             target = lax.rem(quarter_ref[0] + quarters - d, quarters)
-            value = dot_t(downs[d][j], mine)
+            value = dot_t(downs[d][j] if d else downs[0][j, :, own], mine)
             out_ref[target, j * hidden : (j + 1) * hidden, :] = value.astype(BF)
 
 
@@ -265,12 +266,12 @@
 
     received = exchange(slots.reshape(exp_groups, block, piece), "exp")
 
-    downs = []
-    for d in range(quarters):
+    downs = [w_down]
+    for d in range(1, quarters):
         start = lax.rem(quarter[0] + d, quarters) * piece
         own = lax.dynamic_slice_in_dim(w_down, start, piece, 2)
         ring = [(i, (i + d) % quarters) for i in range(quarters)]
-        downs.append(lax.ppermute(own, "seq", ring) if d else own)
+        downs.append(lax.ppermute(own, "seq", ring))
 
     def own_rows(values):
         return lax.dynamic_slice_in_dim(values, quarter[0] * part, part, 0)
@@ -281,8 +282,6 @@
 
     own_grad = own_rows(out_grad)
     pairs = jnp.concatenate([own_rows(layer_input), own_grad[8:], own_grad[:8]], axis=0)
-    pairs = doubled(pairs, heads // 2)
-    downs, pairs = lax.optimization_barrier((downs, pairs))
 
     partial_hidden = call(
         hidden_kernel,
@@ -308,8 +307,7 @@
         jnp.swapaxes(w_up, 1, 2),
     )
     mine = exchange(parts, "seq")
-    if heads > 2:
-        pairs = doubled(pairs, heads // 4)
+    pairs = doubled(pairs, heads // 2)
     mine, pairs = lax.optimization_barrier((mine, pairs))
     summed = call(
         sum_kernel,
@@ -321,7 +319,7 @@
         HB,
     )(mine)
     back = exchange(summed, "exp")
-    step = heads // 8
+    step = heads // 4
     while step > 0:
         pairs = doubled(pairs, step)
         step //= 2

time: 175 us -> 173 us (0.989)
  waiting for transfers between devices: 76.3 us -> 79.3 us
  local copies, waits for them, and re-layouts: 4.52 us -> 1.84 us
  other arithmetic: 2.56 us -> 0.16 us
    ppermute x3, waiting for transfers between devices: 0.01 us -> 14 us  [shards(): downs.append(lax.ppermute(own, 'seq', ring))]
    all_to_all x4, waiting for transfers between devices: 53.3 us -> 43.3 us  [exchange(): return lax.all_to_all(blocks, axis, split_axis=0, concat_axis=0, tiled=True)]
    concatenate x3, other arithmetic: 2.53 us -> 0.12 us  [doubled(): return jnp.concatenate([values, other], axis=0)]
  transfers between devices with their start and end apart: 10 -> 10, of which waited for: 7 -> 10; matrix products, arithmetic and copies ran while one was open for 3% -> 1% of each run, Pallas kernels for 0% -> 0%
where the time goes in v4:
time: 173 us; the launch traced here: 172 us
  waiting for transfers between devices  79.3 us (46%)
  starting transfers between devices  61.7 us (36%)
  blocking collectives  16.7 us (10%)
  Pallas kernels  11.6 us (7%)
  local copies, waits for them, and re-layouts  1.84 us (1%)
    all_to_all x4, waiting for transfers between devices, exchange(): return lax.all_to_all(blocks, axis, split_axis=0, concat_axis=0, tiled=True)  43.3 us
    all_to_all x4, starting transfers between devices, exchange(): return lax.all_to_all(blocks, axis, split_axis=0, concat_axis=0, tiled=True)  35.7 us
    ppermute x3, waiting for transfers between devices, doubled(): other = lax.ppermute(values, 'head', [(i, i ^ step) for i in range(heads)])  22.1 us
    all_to_all x1, blocking collectives, exchange(): return lax.all_to_all(blocks, axis, split_axis=0, concat_axis=0, tiled=True)  16.7 us
    ppermute x3, starting transfers between devices, doubled(): other = lax.ppermute(values, 'head', [(i, i ^ step) for i in range(heads)])  14.6 us
    ppermute x3, waiting for transfers between devices, shards(): downs.append(lax.ppermute(own, 'seq', ring))  14 us
    ppermute x3, starting transfers between devices, shards(): downs.append(lax.ppermute(own, 'seq', ring))  11.4 us
  transfers between devices with their start and end apart: 10, of which 10 were waited for; matrix products, arithmetic and copies ran while one was open for 1% of the time, Pallas kernels for 0%

profile of v4, /device:TPU:8, one launch (start us, length us, event | category | flops | bytes accessed | tf_op | source)
XLA Modules:
  0.0 172.2 jit_solution(1925445064776491926)
XLA Ops:
  0.7 2.6 %shard_map.122 = bf16[4,128,512]{2,1,0:T(8,128)(2,1)} custom-call(s32[1]{0:T(128)} %bitcast.1.quarter_ref, s32[8,48]{1,0:T(8,128)} %bitcast.20, f32[8,48]{1,0:T(8,128)} %bitcast.24, bf16[48,2048]{1,0:T(8,128)(2,1)} %grad_hbm.1), custom_call_target="tpu_custom_call" | custom-call | flops 25165824 | bytes 1048576 | tf_op jit(solution)/shard_map/pallas_call | solution.py:250
  3.3 19.2 %all-to-all-start = ((bf16[32,16,512]{2,1,0:T(8,128)(2,1)}), bf16[32,16,512]{2,1,0:T(8,128)(2,1)S(1)}, u32[]{:S(2)}, u32[]{:S(2)}) async-start(bf16[32,16,512]{2,1,0:T(8,128)(2,1)} %bitcast.23), calls=%async_computation | async-start | bytes 1048576 | tf_op jit(solution)/shard_map/all_to_all | solution.py:226
  22.6 3.4 %collective-permute-start = (bf16[2,192,512]{2,1,0:T(8,128)(2,1)S(1)}, bf16[2,192,512]{2,1,0:T(8,128)(2,1)S(1)}, u32[]{:S(2)}, u32[]{:S(2)}) collective-permute-start(bf16[2,192,512]{2,1,0:T(8,128)(2,1)S(1)} %get-tuple-element.20), channel_id=1, source_target_pairs={{0,256},{256,512},{512,768},{768,0},{1,257},{257,513},{513,769},{7... | collective-permute-start | bytes 1179656 | tf_op jit(solution)/shard_map/ppermute | solution.py:274
  26.0 4.6 %collective-permute-start.1 = (bf16[2,192,512]{2,1,0:T(8,128)(2,1)S(1)}, bf16[2,192,512]{2,1,0:T(8,128)(2,1)S(1)}, u32[]{:S(2)}, u32[]{:S(2)}) collective-permute-start(bf16[2,192,512]{2,1,0:T(8,128)(2,1)S(1)} %get-tuple-element.19), channel_id=1, source_target_pairs={{0,512},{256,768},{512,0},{768,256},{1,513},{257,769},{513,1},{769... | collective-permute-start | bytes 1179656 | tf_op jit(solution)/shard_map/ppermute | solution.py:274
  30.6 3.3 %collective-permute-start.2 = (bf16[2,192,512]{2,1,0:T(8,128)(2,1)S(1)}, bf16[2,192,512]{2,1,0:T(8,128)(2,1)S(1)}, u32[]{:S(2)}, u32[]{:S(2)}) collective-permute-start(bf16[2,192,512]{2,1,0:T(8,128)(2,1)S(1)} %get-tuple-element.18), channel_id=1, source_target_pairs={{0,768},{256,0},{512,256},{768,512},{1,769},{257,1},{513,257},{769... | collective-permute-start | bytes 1179656 | tf_op jit(solution)/shard_map/ppermute | solution.py:274
  34.0 3.0 %collective-permute-done.refs_1_ = bf16[2,192,512]{2,1,0:T(8,128)(2,1)S(1)} collective-permute-done((bf16[2,192,512]{2,1,0:T(8,128)(2,1)S(1)}, bf16[2,192,512]{2,1,0:T(8,128)(2,1)S(1)}, u32[]{:S(2)}, u32[]{:S(2)}) %collective-permute-start) | collective-permute-done | bytes 393248 | tf_op jit(solution)/shard_map/ppermute | solution.py:274
  37.0 9.4 %collective-permute-done.1.refs_2_ = bf16[2,192,512]{2,1,0:T(8,128)(2,1)S(1)} collective-permute-done((bf16[2,192,512]{2,1,0:T(8,128)(2,1)S(1)}, bf16[2,192,512]{2,1,0:T(8,128)(2,1)S(1)}, u32[]{:S(2)}, u32[]{:S(2)}) %collective-permute-start.1) | collective-permute-done | bytes 393248 | tf_op jit(solution)/shard_map/ppermute | solution.py:274
  48.0 8.3 %all-to-all-done.rows_ref = bf16[32,16,512]{2,1,0:T(8,128)(2,1)S(1)} async-done(((bf16[32,16,512]{2,1,0:T(8,128)(2,1)}), bf16[32,16,512]{2,1,0:T(8,128)(2,1)S(1)}, u32[]{:S(2)}, u32[]{:S(2)}) %all-to-all-start) | async-done | bytes 524320 | tf_op jit(solution)/shard_map/all_to_all | solution.py:226
  57.1 16.7 %all_to_all.25.parts_ref = bf16[4,384,256]{2,1,0:T(8,128)(2,1)S(1)} all-to-all(bf16[4,384,256]{2,1,0:T(8,128)(2,1)S(1)} %shard_map.123), channel_id=1, replica_groups=mesh['seq'=4,'exp'=32,'head'=8] {'seq'}, dimensions={0} | all-to-all | bytes 1572864 | tf_op jit(solution)/shard_map/all_to_all | solution.py:226
  73.8 2.3 %shard_map.124 = bf16[4,32,16,512]{3,2,1,0:T(8,128)(2,1)} custom-call(bf16[4,384,256]{2,1,0:T(8,128)(2,1)S(1)} %all_to_all.25.parts_ref, bf16[2,256,192]{2,1,0:T(8,128)(2,1)S(1)} %bitcast.18, bf16[2,256,192]{2,1,0:T(8,128)(2,1)S(1)} %bitcast.19, bf16[2,192,2048]{2,1,0:T(8,128)(2,1)S(1)} %bitcast.15, bf16[2,192,2048]{2,1,0:T(8,128)(2,1)S(1)} %bitcast.16), custom_call_target="tpu_custom_call" | custom-call | flops 805306368 | bytes 6291456 | tf_op jit(solution)/shard_map/pallas_call | solution.py:294
  76.1 3.6 %all-to-all-start.2 = ((bf16[4,32,16,512]{3,2,1,0:T(8,128)(2,1)}), bf16[4,32,16,512]{3,2,1,0:T(8,128)(2,1)S(1)}, u32[]{:S(2)}, u32[]{:S(2)}) async-start(bf16[4,32,16,512]{3,2,1,0:T(8,128)(2,1)} %shard_map.124), calls=%async_computation.2 | async-start | bytes 4194304 | tf_op jit(solution)/shard_map/all_to_all | solution.py:226
  81.4 6.8 %collective-permute-start.3 = (bf16[24,2048]{1,0:T(8,128)(2,1)S(1)}, bf16[24,2048]{1,0:T(8,128)(2,1)S(1)}, u32[]{:S(2)}, u32[]{:S(2)}) collective-permute-start(bf16[24,2048]{1,0:T(8,128)(2,1)S(1)} %pad_maximum_fusion.3), channel_id=1, source_target_pairs={{0,4},{1,5},{2,6},{3,7},{4,0},{5,1},{6,2},{7,3},{8,12},{9,13},{10,... | collective-permute-start | bytes 294920 | tf_op jit(solution)/shard_map/ppermute | solution.py:280
  88.3 4.4 %collective-permute-done.3 = bf16[24,2048]{1,0:T(8,128)(2,1)S(1)} collective-permute-done((bf16[24,2048]{1,0:T(8,128)(2,1)S(1)}, bf16[24,2048]{1,0:T(8,128)(2,1)S(1)}, u32[]{:S(2)}, u32[]{:S(2)}) %collective-permute-start.3) | collective-permute-done | bytes 98336 | tf_op jit(solution)/shard_map/ppermute | solution.py:280
  92.7 12.3 %all-to-all-done.2.parts_ref = bf16[4,32,16,512]{3,2,1,0:T(8,128)(2,1)S(1)} async-done(((bf16[4,32,16,512]{3,2,1,0:T(8,128)(2,1)}), bf16[4,32,16,512]{3,2,1,0:T(8,128)(2,1)S(1)}, u32[]{:S(2)}, u32[]{:S(2)}) %all-to-all-start.2) | async-done | bytes 2097184 | tf_op jit(solution)/shard_map/all_to_all | solution.py:226
  106.0 4.6 %all-to-all-start.3 = ((bf16[32,16,512]{2,1,0:T(8,128)(2,1)}), bf16[32,16,512]{2,1,0:T(8,128)(2,1)}, u32[]{:S(2)}, u32[]{:S(2)}) async-start(bf16[32,16,512]{2,1,0:T(8,128)(2,1)} %shard_map.125), calls=%async_computation.3 | async-start | bytes 1048576 | tf_op jit(solution)/shard_map/all_to_all | solution.py:226
  110.6 4.5 %collective-permute-start.4 = (bf16[48,2048]{1,0:T(8,128)(2,1)S(1)}, bf16[48,2048]{1,0:T(8,128)(2,1)S(1)}, u32[]{:S(2)}, u32[]{:S(2)}) collective-permute-start(bf16[48,2048]{1,0:T(8,128)(2,1)S(1)} %pad_maximum_fusion.2), channel_id=1, source_target_pairs={{0,2},{1,3},{2,0},{3,1},{4,6},{5,7},{6,4},{7,5},{8,10},{9,11},{10,... | collective-permute-start | bytes 589832 | tf_op jit(solution)/shard_map/ppermute | solution.py:280
  115.1 8.5 %collective-permute-done.4 = bf16[48,2048]{1,0:T(8,128)(2,1)S(1)} collective-permute-done((bf16[48,2048]{1,0:T(8,128)(2,1)S(1)}, bf16[48,2048]{1,0:T(8,128)(2,1)S(1)}, u32[]{:S(2)}, u32[]{:S(2)}) %collective-permute-start.4) | collective-permute-done | bytes 196640 | tf_op jit(solution)/shard_map/ppermute | solution.py:280
  123.6 3.3 %collective-permute-start.5 = (bf16[96,2048]{1,0:T(8,128)(2,1)S(1)}, bf16[96,2048]{1,0:T(8,128)(2,1)S(1)}, u32[]{:S(2)}, u32[]{:S(2)}) collective-permute-start(bf16[96,2048]{1,0:T(8,128)(2,1)S(1)} %pad_maximum_fusion.1), channel_id=1, source_target_pairs={{0,1},{1,0},{2,3},{3,2},{4,5},{5,4},{6,7},{7,6},{8,9},{9,8},{10,11... | collective-permute-start | bytes 1179656 | tf_op jit(solution)/shard_map/ppermute | solution.py:280
  127.3 9.2 %collective-permute-done.5 = bf16[96,2048]{1,0:T(8,128)(2,1)S(1)} collective-permute-done((bf16[96,2048]{1,0:T(8,128)(2,1)S(1)}, bf16[96,2048]{1,0:T(8,128)(2,1)S(1)}, u32[]{:S(2)}, u32[]{:S(2)}) %collective-permute-start.5) | collective-permute-done | bytes 393248 | tf_op jit(solution)/shard_map/ppermute | solution.py:280
  136.7 7.9 %all-to-all-done.3 = bf16[32,16,512]{2,1,0:T(8,128)(2,1)} async-done(((bf16[32,16,512]{2,1,0:T(8,128)(2,1)}), bf16[32,16,512]{2,1,0:T(8,128)(2,1)}, u32[]{:S(2)}, u32[]{:S(2)}) %all-to-all-start.3) | async-done | bytes 524320 | tf_op jit(solution)/shard_map/all_to_all | solution.py:226
  144.6 2.2 %shard_map.127 = bf16[4,8,48,128]{3,2,1,0:T(8,128)(2,1)} custom-call(bf16[48,512]{1,0:T(8,128)(2,1)S(1)} %shard_map.126.pick_ref, bf16[512,512]{1,0:T(8,128)(2,1)} %bitcast.9.back_ref), custom_call_target="tpu_custom_call" | custom-call | flops 25165824 | bytes 1048576 | tf_op jit(solution)/shard_map/pallas_call | solution.py:335
  146.8 8.3 %all-to-all-start.4 = ((bf16[32,48,128]{2,1,0:T(8,128)(2,1)}), bf16[32,48,128]{2,1,0:T(8,128)(2,1)S(1)}, u32[]{:S(2)}, u32[]{:S(2)}) async-start(bf16[32,48,128]{2,1,0:T(8,128)(2,1)} %bitcast.10), calls=%async_computation.4 | async-start | bytes 786432 | tf_op jit(solution)/shard_map/all_to_all | solution.py:226
  155.1 14.8 %all-to-all-done.4 = bf16[32,48,128]{2,1,0:T(8,128)(2,1)S(1)} async-done(((bf16[32,48,128]{2,1,0:T(8,128)(2,1)}), bf16[32,48,128]{2,1,0:T(8,128)(2,1)S(1)}, u32[]{:S(2)}, u32[]{:S(2)}) %all-to-all-start.4) | async-done | bytes 393248 | tf_op jit(solution)/shard_map/all_to_all | solution.py:226
  169.9 2.3 %shard_map.128 = (f32[12,1,2048]{2,1,0:T(1,128)}, bf16[96,512]{1,0:T(8,128)(2,1)}) custom-call(s32[1]{0:T(128)} %bitcast.head_ref, bf16[4,8,48,128]{3,2,1,0:T(8,128)(2,1)S(1)} %bitcast.17, bf16[192,2048]{1,0:T(8,128)(2,1)S(1)} %pad_maximum_fusion.pairs_ref, f32[1,2048]{1,0:T(1,128)S(1)} %bitcast.22, bf16[512,2048]{1,0:T(8,128)(2,1)S(1)} %copy-done.2), custom_call_target="tpu_custom_call" | custom-call | flops 268435456 | bytes 4194304 | tf_op jit(solution)/shard_map/pallas_call | solution.py:343
  (30 shorter events, 5.7 us)
Async XLA Ops:
  0.6 80.7 %copy-start = (bf16[48,2048]{1,0:T(8,128)(2,1)S(1)}, bf16[48,2048]{1,0:T(8,128)(2,1)}, u32[]{:S(2)}) copy-start(bf16[48,2048]{1,0:T(8,128)(2,1)} %param.12) | copy-start | bytes 589828
  0.6 21.8 %copy-start.1 = (bf16[2,192,2048]{2,1,0:T(8,128)(2,1)S(1)}, bf16[2,192,2048]{2,1,0:T(8,128)(2,1)}, u32[]{:S(2)}) copy-start(bf16[2,192,2048]{2,1,0:T(8,128)(2,1)} %refs_0_.1) | copy-start | bytes 4718596
  3.3 53.0 %all-to-all-start = ((bf16[32,16,512]{2,1,0:T(8,128)(2,1)}), bf16[32,16,512]{2,1,0:T(8,128)(2,1)S(1)}, u32[]{:S(2)}, u32[]{:S(2)}) async-start(bf16[32,16,512]{2,1,0:T(8,128)(2,1)} %bitcast.23), calls=%async_computation | async-start | bytes 1048576 | tf_op jit(solution)/shard_map/all_to_all | solution.py:226
  22.6 14.4 %collective-permute-start = (bf16[2,192,512]{2,1,0:T(8,128)(2,1)S(1)}, bf16[2,192,512]{2,1,0:T(8,128)(2,1)S(1)}, u32[]{:S(2)}, u32[]{:S(2)}) collective-permute-start(bf16[2,192,512]{2,1,0:T(8,128)(2,1)S(1)} %get-tuple-element.20), channel_id=1, source_target_pairs={{0,256},{256,512},{512,768},{768,0},{1,257},{257,513},{513,769},{7... | collective-permute-start | bytes 1179656 | tf_op jit(solution)/shard_map/ppermute | solution.py:274
  26.0 20.4 %collective-permute-start.1 = (bf16[2,192,512]{2,1,0:T(8,128)(2,1)S(1)}, bf16[2,192,512]{2,1,0:T(8,128)(2,1)S(1)}, u32[]{:S(2)}, u32[]{:S(2)}) collective-permute-start(bf16[2,192,512]{2,1,0:T(8,128)(2,1)S(1)} %get-tuple-element.19), channel_id=1, source_target_pairs={{0,512},{256,768},{512,0},{768,256},{1,513},{257,769},{513,1},{769... | collective-permute-start | bytes 1179656 | tf_op jit(solution)/shard_map/ppermute | solution.py:274
  30.6 17.3 %collective-permute-start.2 = (bf16[2,192,512]{2,1,0:T(8,128)(2,1)S(1)}, bf16[2,192,512]{2,1,0:T(8,128)(2,1)S(1)}, u32[]{:S(2)}, u32[]{:S(2)}) collective-permute-start(bf16[2,192,512]{2,1,0:T(8,128)(2,1)S(1)} %get-tuple-element.18), channel_id=1, source_target_pairs={{0,768},{256,0},{512,256},{768,512},{1,769},{257,1},{513,257},{769... | collective-permute-start | bytes 1179656 | tf_op jit(solution)/shard_map/ppermute | solution.py:274
  56.2 17.5 %copy-start.4 = (bf16[2,2048,192]{1,2,0:T(8,128)(2,1)S(1)}, bf16[2,2048,192]{1,2,0:T(8,128)(2,1)}, u32[]{:S(2)}) copy-start(bf16[2,2048,192]{1,2,0:T(8,128)(2,1)} %param.19) | copy-start | bytes 4718596
  56.2 17.5 %copy-start.5 = (bf16[1,2,32,8,192]{4,3,2,1,0:T(8,128)(2,1)S(1)}, bf16[1,2,32,8,192]{4,3,2,1,0:T(8,128)(2,1)}, u32[]{:S(2)}) copy-start(bf16[1,2,32,8,192]{4,3,2,1,0:T(8,128)(2,1)} %param.16) | copy-start | bytes 589828
  56.2 17.5 %copy-start.6 = (bf16[1,2,32,8,192]{4,3,2,1,0:T(8,128)(2,1)S(1)}, bf16[1,2,32,8,192]{4,3,2,1,0:T(8,128)(2,1)}, u32[]{:S(2)}) copy-start(bf16[1,2,32,8,192]{4,3,2,1,0:T(8,128)(2,1)} %param.17) | copy-start | bytes 589828
  57.1 16.7 %copy-start.3 = (bf16[2,2048,192]{1,2,0:T(8,128)(2,1)S(1)}, bf16[2,2048,192]{1,2,0:T(8,128)(2,1)}, u32[]{:S(2)}) copy-start(bf16[2,2048,192]{1,2,0:T(8,128)(2,1)} %param.18) | copy-start | bytes 4718596
  76.1 28.9 %all-to-all-start.2 = ((bf16[4,32,16,512]{3,2,1,0:T(8,128)(2,1)}), bf16[4,32,16,512]{3,2,1,0:T(8,128)(2,1)S(1)}, u32[]{:S(2)}, u32[]{:S(2)}) async-start(bf16[4,32,16,512]{3,2,1,0:T(8,128)(2,1)} %shard_map.124), calls=%async_computation.2 | async-start | bytes 4194304 | tf_op jit(solution)/shard_map/all_to_all | solution.py:226
  81.4 11.2 %collective-permute-start.3 = (bf16[24,2048]{1,0:T(8,128)(2,1)S(1)}, bf16[24,2048]{1,0:T(8,128)(2,1)S(1)}, u32[]{:S(2)}, u32[]{:S(2)}) collective-permute-start(bf16[24,2048]{1,0:T(8,128)(2,1)S(1)} %pad_maximum_fusion.3), channel_id=1, source_target_pairs={{0,4},{1,5},{2,6},{3,7},{4,0},{5,1},{6,2},{7,3},{8,12},{9,13},{10,... | collective-permute-start | bytes 294920 | tf_op jit(solution)/shard_map/ppermute | solution.py:280
  106.0 20.9 %copy-start.7 = (s32[48,8]{0,1:T(8,128)S(1)}, s32[48,8]{0,1:T(8,128)}, u32[]{:S(2)}) copy-start(s32[48,8]{0,1:T(8,128)} %param.14) | copy-start | bytes 4612
  106.0 38.6 %all-to-all-start.3 = ((bf16[32,16,512]{2,1,0:T(8,128)(2,1)}), bf16[32,16,512]{2,1,0:T(8,128)(2,1)}, u32[]{:S(2)}, u32[]{:S(2)}) async-start(bf16[32,16,512]{2,1,0:T(8,128)(2,1)} %shard_map.125), calls=%async_computation.3 | async-start | bytes 1048576 | tf_op jit(solution)/shard_map/all_to_all | solution.py:226
  110.6 13.0 %collective-permute-start.4 = (bf16[48,2048]{1,0:T(8,128)(2,1)S(1)}, bf16[48,2048]{1,0:T(8,128)(2,1)S(1)}, u32[]{:S(2)}, u32[]{:S(2)}) collective-permute-start(bf16[48,2048]{1,0:T(8,128)(2,1)S(1)} %pad_maximum_fusion.2), channel_id=1, source_target_pairs={{0,2},{1,3},{2,0},{3,1},{4,6},{5,7},{6,4},{7,5},{8,10},{9,11},{10,... | collective-permute-start | bytes 589832 | tf_op jit(solution)/shard_map/ppermute | solution.py:280
  123.6 12.9 %collective-permute-start.5 = (bf16[96,2048]{1,0:T(8,128)(2,1)S(1)}, bf16[96,2048]{1,0:T(8,128)(2,1)S(1)}, u32[]{:S(2)}, u32[]{:S(2)}) collective-permute-start(bf16[96,2048]{1,0:T(8,128)(2,1)S(1)} %pad_maximum_fusion.1), channel_id=1, source_target_pairs={{0,1},{1,0},{2,3},{3,2},{4,5},{5,4},{6,7},{7,6},{8,9},{9,8},{10,11... | collective-permute-start | bytes 1179656 | tf_op jit(solution)/shard_map/ppermute | solution.py:280
  127.3 42.6 %copy-start.2 = (bf16[512,2048]{1,0:T(8,128)(2,1)S(1)}, bf16[512,2048]{1,0:T(8,128)(2,1)}, u32[]{:S(2)}) copy-start(bf16[512,2048]{1,0:T(8,128)(2,1)} %w_ref.1) | copy-start | bytes 6291460
  127.3 42.5 %copy-start.8 = (f32[2048]{0:T(1024)S(1)}, f32[2048]{0:T(1024)}, u32[]{:S(2)}) copy-start(f32[2048]{0:T(1024)} %param.13) | copy-start | bytes 24580
  146.8 23.1 %all-to-all-start.4 = ((bf16[32,48,128]{2,1,0:T(8,128)(2,1)}), bf16[32,48,128]{2,1,0:T(8,128)(2,1)S(1)}, u32[]{:S(2)}, u32[]{:S(2)}) async-start(bf16[32,48,128]{2,1,0:T(8,128)(2,1)} %bitcast.10), calls=%async_computation.4 | async-start | bytes 786432 | tf_op jit(solution)/shard_map/all_to_all | solution.py:226

commit v5 on v4

--- a/solution.py
+++ b/solution.py
@@ -174,7 +174,11 @@
     return turned
 
 
-def finish_kernel(head_ref, moe_ref, pairs_ref, gain_ref, w_ref, resid_ref, grad_ref, moe):
+def finish_kernel(
+    head_ref, moe_ref, near_ref, far_hbm, gain_ref, w_ref, resid_ref, grad_ref, moe, far_ref, sem
+):
+    far_copy = pltpu.make_async_copy(far_hbm, far_ref, sem.at[0])
+    far_copy.start()
     quarters, heads, packed, lanes = moe_ref.shape
     part, _, width = resid_ref.shape
     tiles = packed // part
@@ -192,7 +196,9 @@
         for c in range(quarters):
             start = c * piece + n * lanes
             moe[:, start : start + lanes] = moved[:, c * lanes : (c + 1) * lanes]
-    both = pairs_ref[...].astype(F32).reshape(heads, 2 * part, width)
+    far_copy.wait()
+    halves = [ref[...].astype(F32).reshape(heads // 2, 2 * part, width) for ref in (near_ref, far_ref)]
+    both = jnp.concatenate(halves, axis=0)
     x = both[:, :PAD].reshape(rows, width)
     tail = both[:, 8:PAD].reshape(heads * 8, width)
     tail = pltpu.roll(tail, heads * 8 - (PAD - part), 0).reshape(heads, 8, width)
@@ -320,9 +326,10 @@
     )(mine)
     back = exchange(summed, "exp")
     step = heads // 4
-    while step > 0:
+    while step > 1:
         pairs = doubled(pairs, step)
         step //= 2
+    far = lax.ppermute(pairs, "head", [(i, i ^ 1) for i in range(heads)])
     late_routes, summed = lax.optimization_barrier((routes.T, summed))
     pick = call(
         functools.partial(pick_kernel, capacity),
@@ -331,7 +338,7 @@
         2 * rows * tok_count * tok_count,
         1 << 19,
     )(late_routes)
-    back, pick, pairs = lax.optimization_barrier((back, pick, pairs))
+    back, pick, pairs, far, head = lax.optimization_barrier((back, pick, pairs, far, head))
     combined = call(
         combine_kernel,
         sds((quarters, heads, packed, LANES), BF),
@@ -343,14 +350,15 @@
     resid, head_grad = call(
         finish_kernel,
         [sds((part, 1, width), F32), sds((heads * part, attn), BF)],
-        [SM] + [VM] * 4,
+        [SM, VM, VM, HB, VM, VM],
         2 * heads * PAD * width * attn,
         4 << 20,
-        [pltpu.VMEM((heads * PAD, width), F32)],
+        [pltpu.VMEM((heads * PAD, width), F32), pltpu.VMEM(far.shape, BF), DMA((1,))],
     )(
         head,
         got.reshape(quarters, heads, packed, LANES),
         pairs,
+        far,
         norm_gain[None, :],
         w_out,
     )

time: 173 us -> 171 us (0.988)
  blocking collectives: 16.7 us -> 39.5 us
  waiting for transfers between devices: 79.3 us -> 64.7 us
  starting transfers between devices: 61.7 us -> 52.8 us
    all_to_all x1 -> x2, blocking collectives: 16.7 us -> 39.5 us  [exchange(): return lax.all_to_all(blocks, axis, split_axis=0, concat_axis=0, tiled=True)]
    all_to_all x4 -> x3, waiting for transfers between devices: 43.3 us -> 28.5 us  [exchange(): return lax.all_to_all(blocks, axis, split_axis=0, concat_axis=0, tiled=True)]
    ppermute x0 -> x1, waiting for transfers between devices: none -> 9.36 us  [shards(): far = lax.ppermute(pairs, 'head', [(i, i ^ 1) for i in range(heads)])]
    ppermute x3 -> x2, waiting for transfers between devices: 22.1 us -> 12.9 us  [doubled(): other = lax.ppermute(values, 'head', [(i, i ^ step) for i in range(heads)])]
    all_to_all x4 -> x3, starting transfers between devices: 35.7 us -> 26.8 us  [exchange(): return lax.all_to_all(blocks, axis, split_axis=0, concat_axis=0, tiled=True)]
    ppermute x3 -> x2, starting transfers between devices: 14.6 us -> 11.3 us  [doubled(): other = lax.ppermute(values, 'head', [(i, i ^ step) for i in range(heads)])]
    ppermute x0 -> x1, starting transfers between devices: none -> 3.26 us  [shards(): far = lax.ppermute(pairs, 'head', [(i, i ^ 1) for i in range(heads)])]
    pallas_call x1, Pallas kernels: 2.24 us -> 0.42 us  [shards(): call(combine_kernel, sds((quarters, heads, packed, LANES), BF), [VM] * 2,...]
  transfers between devices with their start and end apart: 10 -> 9, of which waited for: 10 -> 9; matrix products, arithmetic and copies ran while one was open for 1% -> 1% of each run, Pallas kernels for 0% -> 0%
where the time goes in v5:
time: 171 us
  waiting for transfers between devices  64.7 us (38%)
  starting transfers between devices  52.8 us (31%)
  blocking collectives  39.5 us (23%)
  Pallas kernels  10.7 us (6%)
  local copies, waits for them, and re-layouts  1.87 us (1%)
    all_to_all x2, blocking collectives, exchange(): return lax.all_to_all(blocks, axis, split_axis=0, concat_axis=0, tiled=True)  39.5 us
    all_to_all x3, waiting for transfers between devices, exchange(): return lax.all_to_all(blocks, axis, split_axis=0, concat_axis=0, tiled=True)  28.5 us
    all_to_all x3, starting transfers between devices, exchange(): return lax.all_to_all(blocks, axis, split_axis=0, concat_axis=0, tiled=True)  26.8 us
    ppermute x3, waiting for transfers between devices, shards(): downs.append(lax.ppermute(own, 'seq', ring))  14 us
    ppermute x2, waiting for transfers between devices, doubled(): other = lax.ppermute(values, 'head', [(i, i ^ step) for i in range(heads)])  12.9 us
    ppermute x3, starting transfers between devices, shards(): downs.append(lax.ppermute(own, 'seq', ring))  11.4 us
    ppermute x2, starting transfers between devices, doubled(): other = lax.ppermute(values, 'head', [(i, i ^ step) for i in range(heads)])  11.3 us
    ppermute x1, waiting for transfers between devices, shards(): far = lax.ppermute(pairs, 'head', [(i, i ^ 1) for i in range(heads)])  9.36 us
  transfers between devices with their start and end apart: 9, of which 9 were waited for; matrix products, arithmetic and copies ran while one was open for 1% of the time, Pallas kernels for 0%

profile of v5, /device:TPU:8, one launch (start us, length us, event | category | flops | bytes accessed | tf_op | source)
XLA Modules:
  0.0 170.5 jit_solution(8807835643625986047)
XLA Ops:
  0.7 2.6 %shard_map.122 = bf16[4,128,512]{2,1,0:T(8,128)(2,1)} custom-call(s32[1]{0:T(128)} %bitcast.quarter_ref, s32[8,48]{1,0:T(8,128)} %bitcast.22, f32[8,48]{1,0:T(8,128)} %bitcast.26, bf16[48,2048]{1,0:T(8,128)(2,1)} %grad_hbm.1), custom_call_target="tpu_custom_call" | custom-call | flops 25165824 | bytes 1048576 | tf_op jit(solution)/shard_map/pallas_call | solution.py:256
  3.2 19.2 %all-to-all-start = ((bf16[32,16,512]{2,1,0:T(8,128)(2,1)}), bf16[32,16,512]{2,1,0:T(8,128)(2,1)S(1)}, u32[]{:S(2)}, u32[]{:S(2)}) async-start(bf16[32,16,512]{2,1,0:T(8,128)(2,1)} %bitcast.25), calls=%async_computation | async-start | bytes 1048576 | tf_op jit(solution)/shard_map/all_to_all | solution.py:232
  22.6 3.4 %collective-permute-start = (bf16[2,192,512]{2,1,0:T(8,128)(2,1)S(1)}, bf16[2,192,512]{2,1,0:T(8,128)(2,1)S(1)}, u32[]{:S(2)}, u32[]{:S(2)}) collective-permute-start(bf16[2,192,512]{2,1,0:T(8,128)(2,1)S(1)} %get-tuple-element.24), channel_id=1, source_target_pairs={{0,256},{256,512},{512,768},{768,0},{1,257},{257,513},{513,769},{7... | collective-permute-start | bytes 1179656 | tf_op jit(solution)/shard_map/ppermute | solution.py:280
  26.0 4.6 %collective-permute-start.1 = (bf16[2,192,512]{2,1,0:T(8,128)(2,1)S(1)}, bf16[2,192,512]{2,1,0:T(8,128)(2,1)S(1)}, u32[]{:S(2)}, u32[]{:S(2)}) collective-permute-start(bf16[2,192,512]{2,1,0:T(8,128)(2,1)S(1)} %get-tuple-element.23), channel_id=1, source_target_pairs={{0,512},{256,768},{512,0},{768,256},{1,513},{257,769},{513,1},{769... | collective-permute-start | bytes 1179656 | tf_op jit(solution)/shard_map/ppermute | solution.py:280
  30.6 3.3 %collective-permute-start.2 = (bf16[2,192,512]{2,1,0:T(8,128)(2,1)S(1)}, bf16[2,192,512]{2,1,0:T(8,128)(2,1)S(1)}, u32[]{:S(2)}, u32[]{:S(2)}) collective-permute-start(bf16[2,192,512]{2,1,0:T(8,128)(2,1)S(1)} %get-tuple-element.22), channel_id=1, source_target_pairs={{0,768},{256,0},{512,256},{768,512},{1,769},{257,1},{513,257},{769... | collective-permute-start | bytes 1179656 | tf_op jit(solution)/shard_map/ppermute | solution.py:280
  34.0 3.0 %collective-permute-done.refs_1_ = bf16[2,192,512]{2,1,0:T(8,128)(2,1)S(1)} collective-permute-done((bf16[2,192,512]{2,1,0:T(8,128)(2,1)S(1)}, bf16[2,192,512]{2,1,0:T(8,128)(2,1)S(1)}, u32[]{:S(2)}, u32[]{:S(2)}) %collective-permute-start) | collective-permute-done | bytes 393248 | tf_op jit(solution)/shard_map/ppermute | solution.py:280
  37.0 9.4 %collective-permute-done.1.refs_2_ = bf16[2,192,512]{2,1,0:T(8,128)(2,1)S(1)} collective-permute-done((bf16[2,192,512]{2,1,0:T(8,128)(2,1)S(1)}, bf16[2,192,512]{2,1,0:T(8,128)(2,1)S(1)}, u32[]{:S(2)}, u32[]{:S(2)}) %collective-permute-start.1) | collective-permute-done | bytes 393248 | tf_op jit(solution)/shard_map/ppermute | solution.py:280
  46.4 1.6 collective-permute-done.2.refs_3_
  47.9 8.3 %all-to-all-done.rows_ref = bf16[32,16,512]{2,1,0:T(8,128)(2,1)S(1)} async-done(((bf16[32,16,512]{2,1,0:T(8,128)(2,1)}), bf16[32,16,512]{2,1,0:T(8,128)(2,1)S(1)}, u32[]{:S(2)}, u32[]{:S(2)}) %all-to-all-start) | async-done | bytes 524320 | tf_op jit(solution)/shard_map/all_to_all | solution.py:232
  57.1 16.7 %all_to_all.25.parts_ref = bf16[4,384,256]{2,1,0:T(8,128)(2,1)S(1)} all-to-all(bf16[4,384,256]{2,1,0:T(8,128)(2,1)S(1)} %shard_map.123), channel_id=1, replica_groups=mesh['seq'=4,'exp'=32,'head'=8] {'seq'}, dimensions={0} | all-to-all | bytes 1572864 | tf_op jit(solution)/shard_map/all_to_all | solution.py:232
  73.8 2.3 %shard_map.124 = bf16[4,32,16,512]{3,2,1,0:T(8,128)(2,1)} custom-call(bf16[4,384,256]{2,1,0:T(8,128)(2,1)S(1)} %all_to_all.25.parts_ref, bf16[2,256,192]{2,1,0:T(8,128)(2,1)S(1)} %bitcast.20, bf16[2,256,192]{2,1,0:T(8,128)(2,1)S(1)} %bitcast.21, bf16[2,192,2048]{2,1,0:T(8,128)(2,1)S(1)} %bitcast.17, bf16[2,192,2048]{2,1,0:T(8,128)(2,1)S(1)} %bitcast.18), custom_call_target="tpu_custom_call" | custom-call | flops 805306368 | bytes 6291456 | tf_op jit(solution)/shard_map/pallas_call | solution.py:300
  76.1 3.6 %all-to-all-start.2 = ((bf16[4,32,16,512]{3,2,1,0:T(8,128)(2,1)}), bf16[4,32,16,512]{3,2,1,0:T(8,128)(2,1)S(1)}, u32[]{:S(2)}, u32[]{:S(2)}) async-start(bf16[4,32,16,512]{3,2,1,0:T(8,128)(2,1)} %shard_map.124), calls=%async_computation.2 | async-start | bytes 4194304 | tf_op jit(solution)/shard_map/all_to_all | solution.py:232
  81.4 6.8 %collective-permute-start.3 = (bf16[24,2048]{1,0:T(8,128)(2,1)S(1)}, bf16[24,2048]{1,0:T(8,128)(2,1)S(1)}, u32[]{:S(2)}, u32[]{:S(2)}) collective-permute-start(bf16[24,2048]{1,0:T(8,128)(2,1)S(1)} %pad_maximum_fusion.1), channel_id=1, source_target_pairs={{0,4},{1,5},{2,6},{3,7},{4,0},{5,1},{6,2},{7,3},{8,12},{9,13},{10,... | collective-permute-start | bytes 294920 | tf_op jit(solution)/shard_map/ppermute | solution.py:286
  88.3 4.4 %collective-permute-done.3 = bf16[24,2048]{1,0:T(8,128)(2,1)S(1)} collective-permute-done((bf16[24,2048]{1,0:T(8,128)(2,1)S(1)}, bf16[24,2048]{1,0:T(8,128)(2,1)S(1)}, u32[]{:S(2)}, u32[]{:S(2)}) %collective-permute-start.3) | collective-permute-done | bytes 98336 | tf_op jit(solution)/shard_map/ppermute | solution.py:286
  92.7 12.4 %all-to-all-done.2.parts_ref = bf16[4,32,16,512]{3,2,1,0:T(8,128)(2,1)S(1)} async-done(((bf16[4,32,16,512]{3,2,1,0:T(8,128)(2,1)}), bf16[4,32,16,512]{3,2,1,0:T(8,128)(2,1)S(1)}, u32[]{:S(2)}, u32[]{:S(2)}) %all-to-all-start.2) | async-done | bytes 2097184 | tf_op jit(solution)/shard_map/all_to_all | solution.py:232
  105.0 1.0 shard_map.125
  106.0 4.0 %all-to-all-start.3 = ((bf16[32,16,512]{2,1,0:T(8,128)(2,1)}), bf16[32,16,512]{2,1,0:T(8,128)(2,1)S(1)}, u32[]{:S(2)}, u32[]{:S(2)}) async-start(bf16[32,16,512]{2,1,0:T(8,128)(2,1)} %shard_map.125), calls=%async_computation.3 | async-start | bytes 1048576 | tf_op jit(solution)/shard_map/all_to_all | solution.py:232
  110.0 4.5 %collective-permute-start.4 = (bf16[48,2048]{1,0:T(8,128)(2,1)S(1)}, bf16[48,2048]{1,0:T(8,128)(2,1)S(1)}, u32[]{:S(2)}, u32[]{:S(2)}) collective-permute-start(bf16[48,2048]{1,0:T(8,128)(2,1)S(1)} %pad_maximum_fusion), channel_id=1, source_target_pairs={{0,2},{1,3},{2,0},{3,1},{4,6},{5,7},{6,4},{7,5},{8,10},{9,11},{10,... | collective-permute-start | bytes 589832 | tf_op jit(solution)/shard_map/ppermute | solution.py:286
  114.6 8.6 %collective-permute-done.4 = bf16[48,2048]{1,0:T(8,128)(2,1)S(1)} collective-permute-done((bf16[48,2048]{1,0:T(8,128)(2,1)S(1)}, bf16[48,2048]{1,0:T(8,128)(2,1)S(1)}, u32[]{:S(2)}, u32[]{:S(2)}) %collective-permute-start.4) | collective-permute-done | bytes 196640 | tf_op jit(solution)/shard_map/ppermute | solution.py:286
  123.1 3.3 %collective-permute-start.5 = (bf16[96,2048]{1,0:T(8,128)(2,1)S(1)}, bf16[96,2048]{1,0:T(8,128)(2,1)}, u32[]{:S(2)}, u32[]{:S(2)}) collective-permute-start(bf16[96,2048]{1,0:T(8,128)(2,1)S(1)} %constant_dynamic-update-slice_fusion.near_ref), channel_id=1, source_target_pairs={{0,1},{1,0},{2,3},{3,2},{4,5},{5,4},{6,7},{7,6},{8,9},{9,8},{10,11... | collective-permute-start | bytes 1179656 | tf_op jit(solution)/shard_map/ppermute | solution.py:332
  126.8 9.4 %collective-permute-done.5.far_hbm = bf16[96,2048]{1,0:T(8,128)(2,1)} collective-permute-done((bf16[96,2048]{1,0:T(8,128)(2,1)S(1)}, bf16[96,2048]{1,0:T(8,128)(2,1)}, u32[]{:S(2)}, u32[]{:S(2)}) %collective-permute-start.5) | collective-permute-done | bytes 393248 | tf_op jit(solution)/shard_map/ppermute | solution.py:332
  136.2 7.8 %all-to-all-done.3 = bf16[32,16,512]{2,1,0:T(8,128)(2,1)S(1)} async-done(((bf16[32,16,512]{2,1,0:T(8,128)(2,1)}), bf16[32,16,512]{2,1,0:T(8,128)(2,1)S(1)}, u32[]{:S(2)}, u32[]{:S(2)}) %all-to-all-start.3) | async-done | bytes 524320 | tf_op jit(solution)/shard_map/all_to_all | solution.py:232
  144.4 22.9 %all_to_all.26 = bf16[32,48,128]{2,1,0:T(8,128)(2,1)S(1)} all-to-all(bf16[32,48,128]{2,1,0:T(8,128)(2,1)S(1)} %bitcast.16), channel_id=1, replica_groups=mesh['seq'=4,'exp'=32,'head'=8] {'seq','head'}, dimensions={0} | all-to-all | bytes 786432 | tf_op jit(solution)/shard_map/all_to_all | solution.py:232
  167.3 3.2 %shard_map.128 = (f32[12,1,2048]{2,1,0:T(1,128)}, bf16[96,512]{1,0:T(8,128)(2,1)}) custom-call(s32[1]{0:T(128)} %bitcast.8.head_ref, bf16[4,8,48,128]{3,2,1,0:T(8,128)(2,1)S(1)} %bitcast.19, bf16[96,2048]{1,0:T(8,128)(2,1)S(1)} %constant_dynamic-update-slice_fusion.near_ref, bf16[96,2048]{1,0:T(8,128)(2,1)} %collective-permute-done.5.far_hbm, ...), custom_call_target="tpu_custom_call" | custom-call | flops 268435456 | bytes 4194304 | tf_op jit(solution)/shard_map/pallas_call | solution.py:350
  (29 shorter events, 3.6 us)
Async XLA Ops:
  0.6 80.7 %copy-start = (bf16[48,2048]{1,0:T(8,128)(2,1)S(1)}, bf16[48,2048]{1,0:T(8,128)(2,1)}, u32[]{:S(2)}) copy-start(bf16[48,2048]{1,0:T(8,128)(2,1)} %param.12) | copy-start | bytes 589828
  0.6 21.8 %copy-start.1 = (bf16[2,192,2048]{2,1,0:T(8,128)(2,1)S(1)}, bf16[2,192,2048]{2,1,0:T(8,128)(2,1)}, u32[]{:S(2)}) copy-start(bf16[2,192,2048]{2,1,0:T(8,128)(2,1)} %refs_0_.1) | copy-start | bytes 4718596
  3.2 53.0 %all-to-all-start = ((bf16[32,16,512]{2,1,0:T(8,128)(2,1)}), bf16[32,16,512]{2,1,0:T(8,128)(2,1)S(1)}, u32[]{:S(2)}, u32[]{:S(2)}) async-start(bf16[32,16,512]{2,1,0:T(8,128)(2,1)} %bitcast.25), calls=%async_computation | async-start | bytes 1048576 | tf_op jit(solution)/shard_map/all_to_all | solution.py:232
  22.6 14.4 %collective-permute-start = (bf16[2,192,512]{2,1,0:T(8,128)(2,1)S(1)}, bf16[2,192,512]{2,1,0:T(8,128)(2,1)S(1)}, u32[]{:S(2)}, u32[]{:S(2)}) collective-permute-start(bf16[2,192,512]{2,1,0:T(8,128)(2,1)S(1)} %get-tuple-element.24), channel_id=1, source_target_pairs={{0,256},{256,512},{512,768},{768,0},{1,257},{257,513},{513,769},{7... | collective-permute-start | bytes 1179656 | tf_op jit(solution)/shard_map/ppermute | solution.py:280
  26.0 20.4 %collective-permute-start.1 = (bf16[2,192,512]{2,1,0:T(8,128)(2,1)S(1)}, bf16[2,192,512]{2,1,0:T(8,128)(2,1)S(1)}, u32[]{:S(2)}, u32[]{:S(2)}) collective-permute-start(bf16[2,192,512]{2,1,0:T(8,128)(2,1)S(1)} %get-tuple-element.23), channel_id=1, source_target_pairs={{0,512},{256,768},{512,0},{768,256},{1,513},{257,769},{513,1},{769... | collective-permute-start | bytes 1179656 | tf_op jit(solution)/shard_map/ppermute | solution.py:280
  30.6 17.3 %collective-permute-start.2 = (bf16[2,192,512]{2,1,0:T(8,128)(2,1)S(1)}, bf16[2,192,512]{2,1,0:T(8,128)(2,1)S(1)}, u32[]{:S(2)}, u32[]{:S(2)}) collective-permute-start(bf16[2,192,512]{2,1,0:T(8,128)(2,1)S(1)} %get-tuple-element.22), channel_id=1, source_target_pairs={{0,768},{256,0},{512,256},{768,512},{1,769},{257,1},{513,257},{769... | collective-permute-start | bytes 1179656 | tf_op jit(solution)/shard_map/ppermute | solution.py:280
  56.2 17.6 %copy-start.4 = (bf16[2,2048,192]{1,2,0:T(8,128)(2,1)S(1)}, bf16[2,2048,192]{1,2,0:T(8,128)(2,1)}, u32[]{:S(2)}) copy-start(bf16[2,2048,192]{1,2,0:T(8,128)(2,1)} %param.19) | copy-start | bytes 4718596
  56.2 17.6 %copy-start.5 = (bf16[1,2,32,8,192]{4,3,2,1,0:T(8,128)(2,1)S(1)}, bf16[1,2,32,8,192]{4,3,2,1,0:T(8,128)(2,1)}, u32[]{:S(2)}) copy-start(bf16[1,2,32,8,192]{4,3,2,1,0:T(8,128)(2,1)} %param.16) | copy-start | bytes 589828
  56.2 17.6 %copy-start.6 = (bf16[1,2,32,8,192]{4,3,2,1,0:T(8,128)(2,1)S(1)}, bf16[1,2,32,8,192]{4,3,2,1,0:T(8,128)(2,1)}, u32[]{:S(2)}) copy-start(bf16[1,2,32,8,192]{4,3,2,1,0:T(8,128)(2,1)} %param.17) | copy-start | bytes 589828
  57.0 16.7 %copy-start.3 = (bf16[2,2048,192]{1,2,0:T(8,128)(2,1)S(1)}, bf16[2,2048,192]{1,2,0:T(8,128)(2,1)}, u32[]{:S(2)}) copy-start(bf16[2,2048,192]{1,2,0:T(8,128)(2,1)} %param.18) | copy-start | bytes 4718596
  76.1 28.9 %all-to-all-start.2 = ((bf16[4,32,16,512]{3,2,1,0:T(8,128)(2,1)}), bf16[4,32,16,512]{3,2,1,0:T(8,128)(2,1)S(1)}, u32[]{:S(2)}, u32[]{:S(2)}) async-start(bf16[4,32,16,512]{3,2,1,0:T(8,128)(2,1)} %shard_map.124), calls=%async_computation.2 | async-start | bytes 4194304 | tf_op jit(solution)/shard_map/all_to_all | solution.py:232
  81.4 11.2 %collective-permute-start.3 = (bf16[24,2048]{1,0:T(8,128)(2,1)S(1)}, bf16[24,2048]{1,0:T(8,128)(2,1)S(1)}, u32[]{:S(2)}, u32[]{:S(2)}) collective-permute-start(bf16[24,2048]{1,0:T(8,128)(2,1)S(1)} %pad_maximum_fusion.1), channel_id=1, source_target_pairs={{0,4},{1,5},{2,6},{3,7},{4,0},{5,1},{6,2},{7,3},{8,12},{9,13},{10,... | collective-permute-start | bytes 294920 | tf_op jit(solution)/shard_map/ppermute | solution.py:286
  105.0 21.4 %copy-start.7 = (s32[48,8]{0,1:T(8,128)S(1)}, s32[48,8]{0,1:T(8,128)}, u32[]{:S(2)}) copy-start(s32[48,8]{0,1:T(8,128)} %param.14) | copy-start | bytes 4612
  106.0 61.3 %copy-start.2 = (bf16[512,2048]{1,0:T(8,128)(2,1)S(1)}, bf16[512,2048]{1,0:T(8,128)(2,1)}, u32[]{:S(2)}) copy-start(bf16[512,2048]{1,0:T(8,128)(2,1)} %w_ref.1) | copy-start | bytes 6291460
  106.0 61.3 %copy-start.8 = (f32[2048]{0:T(1024)S(1)}, f32[2048]{0:T(1024)}, u32[]{:S(2)}) copy-start(f32[2048]{0:T(1024)} %param.13) | copy-start | bytes 24580
  106.0 38.0 %all-to-all-start.3 = ((bf16[32,16,512]{2,1,0:T(8,128)(2,1)}), bf16[32,16,512]{2,1,0:T(8,128)(2,1)S(1)}, u32[]{:S(2)}, u32[]{:S(2)}) async-start(bf16[32,16,512]{2,1,0:T(8,128)(2,1)} %shard_map.125), calls=%async_computation.3 | async-start | bytes 1048576 | tf_op jit(solution)/shard_map/all_to_all | solution.py:232
  110.0 13.1 %collective-permute-start.4 = (bf16[48,2048]{1,0:T(8,128)(2,1)S(1)}, bf16[48,2048]{1,0:T(8,128)(2,1)S(1)}, u32[]{:S(2)}, u32[]{:S(2)}) collective-permute-start(bf16[48,2048]{1,0:T(8,128)(2,1)S(1)} %pad_maximum_fusion), channel_id=1, source_target_pairs={{0,2},{1,3},{2,0},{3,1},{4,6},{5,7},{6,4},{7,5},{8,10},{9,11},{10,... | collective-permute-start | bytes 589832 | tf_op jit(solution)/shard_map/ppermute | solution.py:286
  123.1 13.0 %collective-permute-start.5 = (bf16[96,2048]{1,0:T(8,128)(2,1)S(1)}, bf16[96,2048]{1,0:T(8,128)(2,1)}, u32[]{:S(2)}, u32[]{:S(2)}) collective-permute-start(bf16[96,2048]{1,0:T(8,128)(2,1)S(1)} %constant_dynamic-update-slice_fusion.near_ref), channel_id=1, source_target_pairs={{0,1},{1,0},{2,3},{3,2},{4,5},{5,4},{6,7},{7,6},{8,9},{9,8},{10,11... | collective-permute-start | bytes 1179656 | tf_op jit(solution)/shard_map/ppermute | solution.py:332

commit v6 on v5

--- a/solution.py
+++ b/solution.py
@@ -175,7 +175,7 @@
 
 
 def finish_kernel(
-    head_ref, moe_ref, near_ref, far_hbm, gain_ref, w_ref, resid_ref, grad_ref, moe, far_ref, sem
+    head_ref, moe_ref, near_ref, far_hbm, gain_ref, w_ref, resid_ref, grad_ref, moe, full, far_ref, sem
 ):
     far_copy = pltpu.make_async_copy(far_hbm, far_ref, sem.at[0])
     far_copy.start()
@@ -196,20 +196,26 @@
         for c in range(quarters):
             start = c * piece + n * lanes
             moe[:, start : start + lanes] = moved[:, c * lanes : (c + 1) * lanes]
-    far_copy.wait()
-    halves = [ref[...].astype(F32).reshape(heads // 2, 2 * part, width) for ref in (near_ref, far_ref)]
-    both = jnp.concatenate(halves, axis=0)
-    x = both[:, :PAD].reshape(rows, width)
-    tail = both[:, 8:PAD].reshape(heads * 8, width)
-    tail = pltpu.roll(tail, heads * 8 - (PAD - part), 0).reshape(heads, 8, width)
-    out_rows = jnp.concatenate([both[:, PAD:], tail], axis=1).reshape(rows, width)
-    inv_rms = lax.rsqrt(jnp.sum(x * x, axis=1, keepdims=True) / width + 1e-06)
-    normed = x * inv_rms
-    scaled = moe[...] * gain_ref[...]
-    mean = jnp.sum(scaled * normed, axis=1, keepdims=True) / width
-    full = out_rows + inv_rms * (scaled - normed * mean)
-    resid_ref[...] = full[:part].reshape(part, 1, width)
-    product = dot_t(full.astype(BF), w_ref[...]).astype(BF)
+    count = heads // 2
+    half = count * PAD
+    for n, pairs_ref in enumerate((near_ref, far_ref)):
+        if n:
+            far_copy.wait()
+        some = slice(n * half, (n + 1) * half)
+        both = pairs_ref[...].astype(F32).reshape(count, 2 * part, width)
+        x = both[:, :PAD].reshape(half, width)
+        tail = both[:, 8:PAD].reshape(count * 8, width)
+        tail = pltpu.roll(tail, count * 8 - (PAD - part), 0).reshape(count, 8, width)
+        out_rows = jnp.concatenate([both[:, PAD:], tail], axis=1).reshape(half, width)
+        inv_rms = lax.rsqrt(jnp.sum(x * x, axis=1, keepdims=True) / width + 1e-06)
+        normed = x * inv_rms
+        scaled = moe[some] * gain_ref[...]
+        mean = jnp.sum(scaled * normed, axis=1, keepdims=True) / width
+        value = out_rows + inv_rms * (scaled - normed * mean)
+        if n == 0:
+            resid_ref[...] = value[:part].reshape(part, 1, width)
+        full[some] = value.astype(BF)
+    product = dot_t(full[...], w_ref[...]).astype(BF)
     want = iota((heads * part, rows), 0)
     have = iota((heads * part, rows), 1)
     keep = one_hot(offset((want // part) ^ me, heads) * PAD + want % part == have)
@@ -353,7 +359,12 @@
         [SM, VM, VM, HB, VM, VM],
         2 * heads * PAD * width * attn,
         4 << 20,
-        [pltpu.VMEM((heads * PAD, width), F32), pltpu.VMEM(far.shape, BF), DMA((1,))],
+        [
+            pltpu.VMEM((heads * PAD, width), F32),
+            pltpu.VMEM((heads * PAD, width), BF),
+            pltpu.VMEM(far.shape, BF),
+            DMA((1,)),
+        ],
     )(
         head,
         got.reshape(quarters, heads, packed, LANES),

time: 171 us -> 171 us (level)
  no operation moved by 1% of the time
where the time goes in v6:
time: 171 us; the launch traced here: 170 us
  waiting for transfers between devices  64.7 us (38%)
  starting transfers between devices  52.8 us (31%)
  blocking collectives  39.5 us (23%)
  Pallas kernels  10.6 us (6%)
  local copies, waits for them, and re-layouts  1.87 us (1%)
    all_to_all x2, blocking collectives, exchange(): return lax.all_to_all(blocks, axis, split_axis=0, concat_axis=0, tiled=True)  39.5 us
    all_to_all x3, waiting for transfers between devices, exchange(): return lax.all_to_all(blocks, axis, split_axis=0, concat_axis=0, tiled=True)  28.5 us
    all_to_all x3, starting transfers between devices, exchange(): return lax.all_to_all(blocks, axis, split_axis=0, concat_axis=0, tiled=True)  26.8 us
    ppermute x3, waiting for transfers between devices, shards(): downs.append(lax.ppermute(own, 'seq', ring))  14 us
    ppermute x2, waiting for transfers between devices, doubled(): other = lax.ppermute(values, 'head', [(i, i ^ step) for i in range(heads)])  12.9 us
    ppermute x3, starting transfers between devices, shards(): downs.append(lax.ppermute(own, 'seq', ring))  11.4 us
    ppermute x2, starting transfers between devices, doubled(): other = lax.ppermute(values, 'head', [(i, i ^ step) for i in range(heads)])  11.3 us
    ppermute x1, waiting for transfers between devices, shards(): far = lax.ppermute(pairs, 'head', [(i, i ^ 1) for i in range(heads)])  9.36 us
  transfers between devices with their start and end apart: 9, of which 9 were waited for; matrix products, arithmetic and copies ran while one was open for 1% of the time, Pallas kernels for 0%

profile of v6, /device:TPU:8, one launch (start us, length us, event | category | flops | bytes accessed | tf_op | source)
XLA Modules:
  0.0 170.4 jit_solution(12064789185448345169)
XLA Ops:
  0.7 2.6 %shard_map.122 = bf16[4,128,512]{2,1,0:T(8,128)(2,1)} custom-call(s32[1]{0:T(128)} %bitcast.quarter_ref, s32[8,48]{1,0:T(8,128)} %bitcast.22, f32[8,48]{1,0:T(8,128)} %bitcast.26, bf16[48,2048]{1,0:T(8,128)(2,1)} %grad_hbm.1), custom_call_target="tpu_custom_call" | custom-call | flops 25165824 | bytes 1048576 | tf_op jit(solution)/shard_map/pallas_call | solution.py:262
  3.2 19.2 %all-to-all-start = ((bf16[32,16,512]{2,1,0:T(8,128)(2,1)}), bf16[32,16,512]{2,1,0:T(8,128)(2,1)S(1)}, u32[]{:S(2)}, u32[]{:S(2)}) async-start(bf16[32,16,512]{2,1,0:T(8,128)(2,1)} %bitcast.25), calls=%async_computation | async-start | bytes 1048576 | tf_op jit(solution)/shard_map/all_to_all | solution.py:238
  22.6 3.4 %collective-permute-start = (bf16[2,192,512]{2,1,0:T(8,128)(2,1)S(1)}, bf16[2,192,512]{2,1,0:T(8,128)(2,1)S(1)}, u32[]{:S(2)}, u32[]{:S(2)}) collective-permute-start(bf16[2,192,512]{2,1,0:T(8,128)(2,1)S(1)} %get-tuple-element.24), channel_id=1, source_target_pairs={{0,256},{256,512},{512,768},{768,0},{1,257},{257,513},{513,769},{7... | collective-permute-start | bytes 1179656 | tf_op jit(solution)/shard_map/ppermute | solution.py:286
  26.0 4.6 %collective-permute-start.1 = (bf16[2,192,512]{2,1,0:T(8,128)(2,1)S(1)}, bf16[2,192,512]{2,1,0:T(8,128)(2,1)S(1)}, u32[]{:S(2)}, u32[]{:S(2)}) collective-permute-start(bf16[2,192,512]{2,1,0:T(8,128)(2,1)S(1)} %get-tuple-element.23), channel_id=1, source_target_pairs={{0,512},{256,768},{512,0},{768,256},{1,513},{257,769},{513,1},{769... | collective-permute-start | bytes 1179656 | tf_op jit(solution)/shard_map/ppermute | solution.py:286
  30.6 3.3 %collective-permute-start.2 = (bf16[2,192,512]{2,1,0:T(8,128)(2,1)S(1)}, bf16[2,192,512]{2,1,0:T(8,128)(2,1)S(1)}, u32[]{:S(2)}, u32[]{:S(2)}) collective-permute-start(bf16[2,192,512]{2,1,0:T(8,128)(2,1)S(1)} %get-tuple-element.22), channel_id=1, source_target_pairs={{0,768},{256,0},{512,256},{768,512},{1,769},{257,1},{513,257},{769... | collective-permute-start | bytes 1179656 | tf_op jit(solution)/shard_map/ppermute | solution.py:286
  34.0 3.0 %collective-permute-done.refs_1_ = bf16[2,192,512]{2,1,0:T(8,128)(2,1)S(1)} collective-permute-done((bf16[2,192,512]{2,1,0:T(8,128)(2,1)S(1)}, bf16[2,192,512]{2,1,0:T(8,128)(2,1)S(1)}, u32[]{:S(2)}, u32[]{:S(2)}) %collective-permute-start) | collective-permute-done | bytes 393248 | tf_op jit(solution)/shard_map/ppermute | solution.py:286
  37.0 9.4 %collective-permute-done.1.refs_2_ = bf16[2,192,512]{2,1,0:T(8,128)(2,1)S(1)} collective-permute-done((bf16[2,192,512]{2,1,0:T(8,128)(2,1)S(1)}, bf16[2,192,512]{2,1,0:T(8,128)(2,1)S(1)}, u32[]{:S(2)}, u32[]{:S(2)}) %collective-permute-start.1) | collective-permute-done | bytes 393248 | tf_op jit(solution)/shard_map/ppermute | solution.py:286
  46.4 1.6 collective-permute-done.2.refs_3_
  47.9 8.3 %all-to-all-done.rows_ref = bf16[32,16,512]{2,1,0:T(8,128)(2,1)S(1)} async-done(((bf16[32,16,512]{2,1,0:T(8,128)(2,1)}), bf16[32,16,512]{2,1,0:T(8,128)(2,1)S(1)}, u32[]{:S(2)}, u32[]{:S(2)}) %all-to-all-start) | async-done | bytes 524320 | tf_op jit(solution)/shard_map/all_to_all | solution.py:238
  57.1 16.7 %all_to_all.25.parts_ref = bf16[4,384,256]{2,1,0:T(8,128)(2,1)S(1)} all-to-all(bf16[4,384,256]{2,1,0:T(8,128)(2,1)S(1)} %shard_map.123), channel_id=1, replica_groups=mesh['seq'=4,'exp'=32,'head'=8] {'seq'}, dimensions={0} | all-to-all | bytes 1572864 | tf_op jit(solution)/shard_map/all_to_all | solution.py:238
  73.8 2.3 %shard_map.124 = bf16[4,32,16,512]{3,2,1,0:T(8,128)(2,1)} custom-call(bf16[4,384,256]{2,1,0:T(8,128)(2,1)S(1)} %all_to_all.25.parts_ref, bf16[2,256,192]{2,1,0:T(8,128)(2,1)S(1)} %bitcast.20, bf16[2,256,192]{2,1,0:T(8,128)(2,1)S(1)} %bitcast.21, bf16[2,192,2048]{2,1,0:T(8,128)(2,1)S(1)} %bitcast.17, bf16[2,192,2048]{2,1,0:T(8,128)(2,1)S(1)} %bitcast.18), custom_call_target="tpu_custom_call" | custom-call | flops 805306368 | bytes 6291456 | tf_op jit(solution)/shard_map/pallas_call | solution.py:306
  76.1 3.6 %all-to-all-start.2 = ((bf16[4,32,16,512]{3,2,1,0:T(8,128)(2,1)}), bf16[4,32,16,512]{3,2,1,0:T(8,128)(2,1)S(1)}, u32[]{:S(2)}, u32[]{:S(2)}) async-start(bf16[4,32,16,512]{3,2,1,0:T(8,128)(2,1)} %shard_map.124), calls=%async_computation.2 | async-start | bytes 4194304 | tf_op jit(solution)/shard_map/all_to_all | solution.py:238
  81.4 6.8 %collective-permute-start.3 = (bf16[24,2048]{1,0:T(8,128)(2,1)S(1)}, bf16[24,2048]{1,0:T(8,128)(2,1)S(1)}, u32[]{:S(2)}, u32[]{:S(2)}) collective-permute-start(bf16[24,2048]{1,0:T(8,128)(2,1)S(1)} %pad_maximum_fusion.1), channel_id=1, source_target_pairs={{0,4},{1,5},{2,6},{3,7},{4,0},{5,1},{6,2},{7,3},{8,12},{9,13},{10,... | collective-permute-start | bytes 294920 | tf_op jit(solution)/shard_map/ppermute | solution.py:292
  88.3 4.4 %collective-permute-done.3 = bf16[24,2048]{1,0:T(8,128)(2,1)S(1)} collective-permute-done((bf16[24,2048]{1,0:T(8,128)(2,1)S(1)}, bf16[24,2048]{1,0:T(8,128)(2,1)S(1)}, u32[]{:S(2)}, u32[]{:S(2)}) %collective-permute-start.3) | collective-permute-done | bytes 98336 | tf_op jit(solution)/shard_map/ppermute | solution.py:292
  92.7 12.4 %all-to-all-done.2.parts_ref = bf16[4,32,16,512]{3,2,1,0:T(8,128)(2,1)S(1)} async-done(((bf16[4,32,16,512]{3,2,1,0:T(8,128)(2,1)}), bf16[4,32,16,512]{3,2,1,0:T(8,128)(2,1)S(1)}, u32[]{:S(2)}, u32[]{:S(2)}) %all-to-all-start.2) | async-done | bytes 2097184 | tf_op jit(solution)/shard_map/all_to_all | solution.py:238
  105.0 1.0 shard_map.125
  106.0 4.0 %all-to-all-start.3 = ((bf16[32,16,512]{2,1,0:T(8,128)(2,1)}), bf16[32,16,512]{2,1,0:T(8,128)(2,1)S(1)}, u32[]{:S(2)}, u32[]{:S(2)}) async-start(bf16[32,16,512]{2,1,0:T(8,128)(2,1)} %shard_map.125), calls=%async_computation.3 | async-start | bytes 1048576 | tf_op jit(solution)/shard_map/all_to_all | solution.py:238
  110.0 4.5 %collective-permute-start.4 = (bf16[48,2048]{1,0:T(8,128)(2,1)S(1)}, bf16[48,2048]{1,0:T(8,128)(2,1)S(1)}, u32[]{:S(2)}, u32[]{:S(2)}) collective-permute-start(bf16[48,2048]{1,0:T(8,128)(2,1)S(1)} %pad_maximum_fusion), channel_id=1, source_target_pairs={{0,2},{1,3},{2,0},{3,1},{4,6},{5,7},{6,4},{7,5},{8,10},{9,11},{10,... | collective-permute-start | bytes 589832 | tf_op jit(solution)/shard_map/ppermute | solution.py:292
  114.6 8.6 %collective-permute-done.4 = bf16[48,2048]{1,0:T(8,128)(2,1)S(1)} collective-permute-done((bf16[48,2048]{1,0:T(8,128)(2,1)S(1)}, bf16[48,2048]{1,0:T(8,128)(2,1)S(1)}, u32[]{:S(2)}, u32[]{:S(2)}) %collective-permute-start.4) | collective-permute-done | bytes 196640 | tf_op jit(solution)/shard_map/ppermute | solution.py:292
  123.1 3.3 %collective-permute-start.5 = (bf16[96,2048]{1,0:T(8,128)(2,1)S(1)}, bf16[96,2048]{1,0:T(8,128)(2,1)}, u32[]{:S(2)}, u32[]{:S(2)}) collective-permute-start(bf16[96,2048]{1,0:T(8,128)(2,1)S(1)} %constant_dynamic-update-slice_fusion.near_ref), channel_id=1, source_target_pairs={{0,1},{1,0},{2,3},{3,2},{4,5},{5,4},{6,7},{7,6},{8,9},{9,8},{10,11... | collective-permute-start | bytes 1179656 | tf_op jit(solution)/shard_map/ppermute | solution.py:338
  126.8 9.4 %collective-permute-done.5.far_hbm = bf16[96,2048]{1,0:T(8,128)(2,1)} collective-permute-done((bf16[96,2048]{1,0:T(8,128)(2,1)S(1)}, bf16[96,2048]{1,0:T(8,128)(2,1)}, u32[]{:S(2)}, u32[]{:S(2)}) %collective-permute-start.5) | collective-permute-done | bytes 393248 | tf_op jit(solution)/shard_map/ppermute | solution.py:338
  136.2 7.8 %all-to-all-done.3 = bf16[32,16,512]{2,1,0:T(8,128)(2,1)S(1)} async-done(((bf16[32,16,512]{2,1,0:T(8,128)(2,1)}), bf16[32,16,512]{2,1,0:T(8,128)(2,1)S(1)}, u32[]{:S(2)}, u32[]{:S(2)}) %all-to-all-start.3) | async-done | bytes 524320 | tf_op jit(solution)/shard_map/all_to_all | solution.py:238
  144.4 22.9 %all_to_all.26 = bf16[32,48,128]{2,1,0:T(8,128)(2,1)S(1)} all-to-all(bf16[32,48,128]{2,1,0:T(8,128)(2,1)S(1)} %bitcast.16), channel_id=1, replica_groups=mesh['seq'=4,'exp'=32,'head'=8] {'seq','head'}, dimensions={0} | all-to-all | bytes 786432 | tf_op jit(solution)/shard_map/all_to_all | solution.py:238
  167.3 3.1 %shard_map.128 = (f32[12,1,2048]{2,1,0:T(1,128)}, bf16[96,512]{1,0:T(8,128)(2,1)}) custom-call(s32[1]{0:T(128)} %bitcast.8.head_ref, bf16[4,8,48,128]{3,2,1,0:T(8,128)(2,1)S(1)} %bitcast.19, bf16[96,2048]{1,0:T(8,128)(2,1)S(1)} %constant_dynamic-update-slice_fusion.near_ref, bf16[96,2048]{1,0:T(8,128)(2,1)} %collective-permute-done.5.far_hbm, ...), custom_call_target="tpu_custom_call" | custom-call | flops 268435456 | bytes 4194304 | tf_op jit(solution)/shard_map/pallas_call | solution.py:356
  (29 shorter events, 3.6 us)
Async XLA Ops:
  0.6 80.7 %copy-start = (bf16[48,2048]{1,0:T(8,128)(2,1)S(1)}, bf16[48,2048]{1,0:T(8,128)(2,1)}, u32[]{:S(2)}) copy-start(bf16[48,2048]{1,0:T(8,128)(2,1)} %param.12) | copy-start | bytes 589828
  0.6 21.8 %copy-start.1 = (bf16[2,192,2048]{2,1,0:T(8,128)(2,1)S(1)}, bf16[2,192,2048]{2,1,0:T(8,128)(2,1)}, u32[]{:S(2)}) copy-start(bf16[2,192,2048]{2,1,0:T(8,128)(2,1)} %refs_0_.1) | copy-start | bytes 4718596
  3.2 53.0 %all-to-all-start = ((bf16[32,16,512]{2,1,0:T(8,128)(2,1)}), bf16[32,16,512]{2,1,0:T(8,128)(2,1)S(1)}, u32[]{:S(2)}, u32[]{:S(2)}) async-start(bf16[32,16,512]{2,1,0:T(8,128)(2,1)} %bitcast.25), calls=%async_computation | async-start | bytes 1048576 | tf_op jit(solution)/shard_map/all_to_all | solution.py:238
  22.6 14.4 %collective-permute-start = (bf16[2,192,512]{2,1,0:T(8,128)(2,1)S(1)}, bf16[2,192,512]{2,1,0:T(8,128)(2,1)S(1)}, u32[]{:S(2)}, u32[]{:S(2)}) collective-permute-start(bf16[2,192,512]{2,1,0:T(8,128)(2,1)S(1)} %get-tuple-element.24), channel_id=1, source_target_pairs={{0,256},{256,512},{512,768},{768,0},{1,257},{257,513},{513,769},{7... | collective-permute-start | bytes 1179656 | tf_op jit(solution)/shard_map/ppermute | solution.py:286
  26.0 20.4 %collective-permute-start.1 = (bf16[2,192,512]{2,1,0:T(8,128)(2,1)S(1)}, bf16[2,192,512]{2,1,0:T(8,128)(2,1)S(1)}, u32[]{:S(2)}, u32[]{:S(2)}) collective-permute-start(bf16[2,192,512]{2,1,0:T(8,128)(2,1)S(1)} %get-tuple-element.23), channel_id=1, source_target_pairs={{0,512},{256,768},{512,0},{768,256},{1,513},{257,769},{513,1},{769... | collective-permute-start | bytes 1179656 | tf_op jit(solution)/shard_map/ppermute | solution.py:286
  30.6 17.3 %collective-permute-start.2 = (bf16[2,192,512]{2,1,0:T(8,128)(2,1)S(1)}, bf16[2,192,512]{2,1,0:T(8,128)(2,1)S(1)}, u32[]{:S(2)}, u32[]{:S(2)}) collective-permute-start(bf16[2,192,512]{2,1,0:T(8,128)(2,1)S(1)} %get-tuple-element.22), channel_id=1, source_target_pairs={{0,768},{256,0},{512,256},{768,512},{1,769},{257,1},{513,257},{769... | collective-permute-start | bytes 1179656 | tf_op jit(solution)/shard_map/ppermute | solution.py:286
  56.2 17.6 %copy-start.4 = (bf16[2,2048,192]{1,2,0:T(8,128)(2,1)S(1)}, bf16[2,2048,192]{1,2,0:T(8,128)(2,1)}, u32[]{:S(2)}) copy-start(bf16[2,2048,192]{1,2,0:T(8,128)(2,1)} %param.19) | copy-start | bytes 4718596
  56.2 17.6 %copy-start.5 = (bf16[1,2,32,8,192]{4,3,2,1,0:T(8,128)(2,1)S(1)}, bf16[1,2,32,8,192]{4,3,2,1,0:T(8,128)(2,1)}, u32[]{:S(2)}) copy-start(bf16[1,2,32,8,192]{4,3,2,1,0:T(8,128)(2,1)} %param.16) | copy-start | bytes 589828
  56.2 17.6 %copy-start.6 = (bf16[1,2,32,8,192]{4,3,2,1,0:T(8,128)(2,1)S(1)}, bf16[1,2,32,8,192]{4,3,2,1,0:T(8,128)(2,1)}, u32[]{:S(2)}) copy-start(bf16[1,2,32,8,192]{4,3,2,1,0:T(8,128)(2,1)} %param.17) | copy-start | bytes 589828
  57.0 16.7 %copy-start.3 = (bf16[2,2048,192]{1,2,0:T(8,128)(2,1)S(1)}, bf16[2,2048,192]{1,2,0:T(8,128)(2,1)}, u32[]{:S(2)}) copy-start(bf16[2,2048,192]{1,2,0:T(8,128)(2,1)} %param.18) | copy-start | bytes 4718596
  76.1 28.9 %all-to-all-start.2 = ((bf16[4,32,16,512]{3,2,1,0:T(8,128)(2,1)}), bf16[4,32,16,512]{3,2,1,0:T(8,128)(2,1)S(1)}, u32[]{:S(2)}, u32[]{:S(2)}) async-start(bf16[4,32,16,512]{3,2,1,0:T(8,128)(2,1)} %shard_map.124), calls=%async_computation.2 | async-start | bytes 4194304 | tf_op jit(solution)/shard_map/all_to_all | solution.py:238
  81.4 11.2 %collective-permute-start.3 = (bf16[24,2048]{1,0:T(8,128)(2,1)S(1)}, bf16[24,2048]{1,0:T(8,128)(2,1)S(1)}, u32[]{:S(2)}, u32[]{:S(2)}) collective-permute-start(bf16[24,2048]{1,0:T(8,128)(2,1)S(1)} %pad_maximum_fusion.1), channel_id=1, source_target_pairs={{0,4},{1,5},{2,6},{3,7},{4,0},{5,1},{6,2},{7,3},{8,12},{9,13},{10,... | collective-permute-start | bytes 294920 | tf_op jit(solution)/shard_map/ppermute | solution.py:292
  105.0 21.4 %copy-start.7 = (s32[48,8]{0,1:T(8,128)S(1)}, s32[48,8]{0,1:T(8,128)}, u32[]{:S(2)}) copy-start(s32[48,8]{0,1:T(8,128)} %param.14) | copy-start | bytes 4612
  106.0 61.3 %copy-start.2 = (bf16[512,2048]{1,0:T(8,128)(2,1)S(1)}, bf16[512,2048]{1,0:T(8,128)(2,1)}, u32[]{:S(2)}) copy-start(bf16[512,2048]{1,0:T(8,128)(2,1)} %w_ref.1) | copy-start | bytes 6291460
  106.0 61.3 %copy-start.8 = (f32[2048]{0:T(1024)S(1)}, f32[2048]{0:T(1024)}, u32[]{:S(2)}) copy-start(f32[2048]{0:T(1024)} %param.13) | copy-start | bytes 24580
  106.0 38.0 %all-to-all-start.3 = ((bf16[32,16,512]{2,1,0:T(8,128)(2,1)}), bf16[32,16,512]{2,1,0:T(8,128)(2,1)S(1)}, u32[]{:S(2)}, u32[]{:S(2)}) async-start(bf16[32,16,512]{2,1,0:T(8,128)(2,1)} %shard_map.125), calls=%async_computation.3 | async-start | bytes 1048576 | tf_op jit(solution)/shard_map/all_to_all | solution.py:238
  110.0 13.1 %collective-permute-start.4 = (bf16[48,2048]{1,0:T(8,128)(2,1)S(1)}, bf16[48,2048]{1,0:T(8,128)(2,1)S(1)}, u32[]{:S(2)}, u32[]{:S(2)}) collective-permute-start(bf16[48,2048]{1,0:T(8,128)(2,1)S(1)} %pad_maximum_fusion), channel_id=1, source_target_pairs={{0,2},{1,3},{2,0},{3,1},{4,6},{5,7},{6,4},{7,5},{8,10},{9,11},{10,... | collective-permute-start | bytes 589832 | tf_op jit(solution)/shard_map/ppermute | solution.py:292
  123.1 13.0 %collective-permute-start.5 = (bf16[96,2048]{1,0:T(8,128)(2,1)S(1)}, bf16[96,2048]{1,0:T(8,128)(2,1)}, u32[]{:S(2)}, u32[]{:S(2)}) collective-permute-start(bf16[96,2048]{1,0:T(8,128)(2,1)S(1)} %constant_dynamic-update-slice_fusion.near_ref), channel_id=1, source_target_pairs={{0,1},{1,0},{2,3},{3,2},{4,5},{5,4},{6,7},{7,6},{8,9},{9,8},{10,11... | collective-permute-start | bytes 1179656 | tf_op jit(solution)/shard_map/ppermute | solution.py:338
